TPU v7x, 32 devices: a whole 2x2x4 slice. The times are simulated.
32 devices in a mesh: section: 2 (over core), ctx: 4 (over z), fsdp: 4 (over y, x).
Axes of the slice: x: 2, y: 2, z: 4, core: 2. Of those that a mesh axis runs over, the one named last changes fastest.
Arguments:
- block_input: bfloat16 [24, 1024, 768], P('fsdp', 'ctx'), may hold values from -6 to 6
- positions: int32 [24, 1024], P('fsdp'), may hold values from 0 to 1023, each once within a row
- cotangent: bfloat16 [24, 1024, 768], P('fsdp', 'ctx'), may hold values from -6 to 6
- w_qkv: bfloat16 [2, 768, 2304], P('section', 'fsdp'), may hold values from -0.21875 to 0.21875
- w_proj: bfloat16 [2, 768, 768], P('section', 'fsdp'), may hold values from -1.25 to 1.25
- w_fc: bfloat16 [2, 768, 3072], P('section', 'fsdp'), may hold values from -0.21875 to 0.21875
- w_out: bfloat16 [2, 3072, 768], P('section', 'fsdp'), may hold values from -0.109375 to 0.109375
- ln_gain: bfloat16 [2, 2, 768], P('section', None, 'fsdp'), may hold values from 0.099609375 to 1.8984375
- ln_bias: bfloat16 [2, 2, 768], P('section', None, 'fsdp'), may hold values from -1.75 to 1.75
- attn_bias: bfloat16 [2, 2, 768], P('section', None, 'fsdp'), may hold values from -3 to 3
- out_bias: bfloat16 [2, 2, 768], P('section', None, 'fsdp'), may hold values from -1.75 to 1.75
- fc_bias: bfloat16 [2, 3072], P('section', 'fsdp'), may hold values from -3 to 3
Outputs:
- section_out: bfloat16 [2, 24, 1024, 768], P('section', 'fsdp', 'ctx')
- section_in_grad: bfloat16 [2, 24, 1024, 768], P('section', 'fsdp', 'ctx')
- grad_w_qkv: float32 [2, 768, 2304], P('section', 'fsdp')
- grad_w_proj: float32 [2, 768, 768], P('section', 'fsdp')
- grad_w_fc: float32 [2, 768, 3072], P('section', 'fsdp')
- grad_w_out: float32 [2, 3072, 768], P('section', 'fsdp')
- grad_ln_gain: float32 [2, 2, 768], P('section', None, 'fsdp')
- grad_ln_bias: float32 [2, 2, 768], P('section', None, 'fsdp')
- grad_attn_bias: float32 [2, 2, 768], P('section', None, 'fsdp')
- grad_out_bias: float32 [2, 2, 768], P('section', None, 'fsdp')
- grad_fc_bias: float32 [2, 3072], P('section', 'fsdp')
Inputs may be any that keep to these rules, and one draw needn't show every extreme that they name: `positions`: each row is a permutation of the places 0 to 1023 of one sequence.
All inputs are finite; a program needn't handle non-finite values.
Results may differ from a plain program's by a relative error of at most 0.034.
Values may be sent and summed in bfloat16 or wider, within the bound.
A program may use at most 320 MiB of HBM per device.

v0:
```python
import jax
import jax.numpy as jnp
from jax import lax
from jax.sharding import PartitionSpec as P

H = 12
HD = 64
MB_SEQ = 2


masked_score = -1e30
norm_eps = 1e-05


def shifted(value, axis, steps):
    count = lax.axis_size(axis)
    leading, last = (max(0, -steps), min(count, count - steps))
    return lax.ppermute(value, axis, [(source, source + steps) for source in range(leading, last)])


def layer_norm(hidden, gain, offset):
    center = hidden - jnp.mean(hidden, axis=-1, keepdims=True)
    spread = jnp.mean(center * center, axis=-1, keepdims=True)
    return center * lax.rsqrt(spread + norm_eps) * gain + offset


def gelu_tanh(inputs):
    return jax.nn.gelu(inputs, approximate=True)


def split_heads(rows):
    return rows.reshape(rows.shape[0], rows.shape[1], H, HD)


def flatten(rows):
    return rows.reshape(-1, rows.shape[-1])


def outer_sum(left, right):
    return jnp.einsum(
        "td,te->de", flatten(left), flatten(right), preferred_element_type=jnp.float32
    )


def project_rows(rows, matrix):
    return jnp.einsum("bsd,de->bse", rows, matrix, preferred_element_type=jnp.float32)


def project_back(grads, matrix):
    return jnp.einsum("bse,de->bsd", grads, matrix, preferred_element_type=jnp.float32)


def token_sum(rows):
    return jnp.sum(rows.astype(jnp.float32), axis=(0, 1))


def front_half(params, hidden):
    w_qkv, w_proj, w_fc, w_out, gains, offsets, attn_bias, out_bias, fc_bias = params
    width = hidden.shape[-1]
    normed = layer_norm(
        hidden, gains[0].astype(jnp.float32), offsets[0].astype(jnp.float32)
    ).astype(jnp.bfloat16)
    project = project_rows(normed, w_qkv)
    queries = (project[..., :width] + attn_bias[0].astype(jnp.float32)).astype(jnp.bfloat16)
    key_rows = project[..., width : 2 * width].astype(jnp.bfloat16)
    value_rows = (project[..., 2 * width :] + attn_bias[1].astype(jnp.float32)).astype(jnp.bfloat16)
    return (normed, queries, key_rows, value_rows)


def back_half(params, hidden, mixed):
    w_qkv, w_proj, w_fc, w_out, gains, offsets, attn_bias, out_bias, fc_bias = params
    after = hidden + project_rows(mixed, w_proj) + out_bias[0].astype(jnp.float32)
    normed_two = layer_norm(
        after, gains[1].astype(jnp.float32), offsets[1].astype(jnp.float32)
    ).astype(jnp.bfloat16)
    inner = project_rows(normed_two, w_fc) + fc_bias.astype(jnp.float32)
    active = gelu_tanh(inner).astype(jnp.bfloat16)
    result = after + project_rows(active, w_out) + out_bias[1].astype(jnp.float32)
    return (after, normed_two, inner, active, result)


def attend_forward(queries, key_rows, value_rows, pos_seq, pos_query):
    batch_seqs, local_rows, width = queries.shape
    scale_factor = HD ** (-0.5)
    query_heads = split_heads(queries)
    running_max = jnp.full((batch_seqs, H, local_rows), masked_score, jnp.float32)
    key_piece = lax.all_gather(key_rows, "ctx", axis=1, tiled=True)
    value_piece = lax.all_gather(value_rows, "ctx", axis=1, tiled=True)
    scores = (
        jnp.einsum(
            "bqhd,bkhd->bhqk",
            query_heads,
            split_heads(key_piece),
            preferred_element_type=jnp.float32,
        )
        * scale_factor
    )
    allowed = pos_query[:, None, :, None] >= pos_seq[:, None, None, :]
    scores = jnp.where(allowed, scores, masked_score)
    new_max = jnp.maximum(running_max, jnp.max(scores, axis=-1))
    weights = jnp.where(allowed, jnp.exp(scores - new_max[..., None]), 0.0)
    running_sum = jnp.sum(weights, axis=-1)
    update = jnp.einsum(
        "bhqk,bkhd->bqhd",
        weights.astype(jnp.bfloat16),
        split_heads(value_piece),
        preferred_element_type=jnp.float32,
    )
    running_out = update
    running_max, running_sum, running_out = (new_max, running_sum, running_out)
    mixed = (running_out / jnp.transpose(running_sum, (0, 2, 1))[..., None]).reshape(
        batch_seqs, local_rows, width
    )
    return (mixed, running_max + jnp.log(running_sum))


def prob_block(query_heads, key_heads, query_places, key_places, log_rows):
    scores = jnp.einsum(
        "bqhd,bkhd->bhqk", query_heads, key_heads, preferred_element_type=jnp.float32
    ) * HD ** (-0.5)
    allowed = query_places[:, None, :, None] >= key_places[:, None, None, :]
    return jnp.where(allowed, jnp.exp(scores - log_rows[..., None]), 0.0)


def score_grads(probs, grad_heads, value_heads, delta_rows):
    grad_probs = jnp.einsum(
        "bqhd,bkhd->bhqk", grad_heads, value_heads, preferred_element_type=jnp.float32
    )
    return (probs * (grad_probs - delta_rows[..., None])).astype(jnp.bfloat16)


def attend_back(queries, key_rows, value_rows, grad_mixed, mixed, log_total, pos_seq, pos_query):
    batch_seqs, local_rows, width = queries.shape
    scale_factor = HD ** (-0.5)
    query_heads = split_heads(queries)
    grad_heads = split_heads(grad_mixed)
    delta = jnp.transpose(
        jnp.sum(split_heads(grad_mixed.astype(jnp.float32) * mixed.astype(jnp.float32)), axis=-1),
        (0, 2, 1),
    )
    key_piece = lax.all_gather(key_rows, "ctx", axis=1, tiled=True)
    value_piece = lax.all_gather(value_rows, "ctx", axis=1, tiled=True)
    count_rows = key_piece.shape[1]
    key_heads = split_heads(key_piece)
    value_heads = split_heads(value_piece)
    probs = prob_block(query_heads, key_heads, pos_query, pos_seq, log_total)
    grad_scores = score_grads(probs, grad_heads, value_heads, delta)
    grad_query = scale_factor * jnp.einsum(
        "bhqk,bkhd->bqhd", grad_scores, key_heads, preferred_element_type=jnp.float32
    )
    probs, grad_scores, grad_query, count_rows = (probs, grad_scores, grad_query, count_rows)
    grad_key = scale_factor * jnp.einsum(
        "bhqk,bqhd->bkhd", grad_scores, query_heads, preferred_element_type=jnp.float32
    )
    grad_value = jnp.einsum(
        "bhqk,bqhd->bkhd",
        probs.astype(jnp.bfloat16),
        grad_heads,
        preferred_element_type=jnp.float32,
    )
    joined = jnp.concatenate(
        [
            grad_key.reshape(batch_seqs, count_rows, width),
            grad_value.reshape(batch_seqs, count_rows, width),
        ],
        axis=-1,
    )
    grad_q = grad_query
    both_grads = lax.psum_scatter(
        joined.astype(jnp.bfloat16), "ctx", scatter_dimension=1, tiled=True
    ).astype(jnp.float32)
    grad_k = both_grads[..., :width].astype(jnp.bfloat16)
    grad_v = both_grads[..., width:].astype(jnp.bfloat16)
    grad_q = grad_q.reshape(batch_seqs, local_rows, width).astype(jnp.bfloat16)
    return (grad_q, grad_k, grad_v)


def layer_back(params, layer_in, mixed, log_total, grad_out, pos_seq, pos_query):
    w_qkv, w_proj, w_fc, w_out, gains, offsets, attn_bias, out_bias, fc_bias = params
    hidden = layer_in.astype(jnp.float32)
    normed, queries, key_rows, value_rows = front_half(params, hidden)
    after, normed_two, inner, active, result = back_half(params, hidden, mixed)
    grad_result = grad_out.astype(jnp.float32)
    grad_w_out = outer_sum(active, grad_out)
    grad_bias_two = token_sum(grad_out)
    grad_active = project_back(grad_out, w_out)
    gelu_value, gelu_pull = jax.vjp(gelu_tanh, inner)
    grad_inner = gelu_pull(grad_active)[0].astype(jnp.bfloat16)
    grad_w_fc = outer_sum(normed_two, grad_inner)
    grad_fc_bias = token_sum(grad_inner)
    grad_normed_two = project_back(grad_inner, w_fc)
    norm_value, norm_pull = jax.vjp(
        layer_norm, after, gains[1].astype(jnp.float32), offsets[1].astype(jnp.float32)
    )
    grad_after, grad_gain_two, grad_offset_two = norm_pull(grad_normed_two)
    grad_after = grad_after + grad_result
    grad_branch = grad_after.astype(jnp.bfloat16)
    grad_w_proj = outer_sum(mixed, grad_branch)
    grad_bias_one = token_sum(grad_branch)
    grad_mixed = project_back(grad_branch, w_proj).astype(jnp.bfloat16)
    grad_q, grad_k, grad_v = attend_back(
        queries, key_rows, value_rows, grad_mixed, mixed, log_total, pos_seq, pos_query
    )
    grad_project = jnp.concatenate([grad_q, grad_k, grad_v], axis=-1)
    grad_w_qkv = outer_sum(normed, grad_project)
    grad_attn = jnp.stack([token_sum(grad_q), token_sum(grad_v)])
    grad_normed = project_back(grad_project, w_qkv)
    first_value, first_pull = jax.vjp(
        layer_norm, hidden, gains[0].astype(jnp.float32), offsets[0].astype(jnp.float32)
    )
    grad_hidden, grad_gain_one, grad_offset_one = first_pull(grad_normed)
    grad_input = (grad_after + grad_hidden).astype(jnp.bfloat16)
    grads = (
        grad_w_qkv,
        grad_w_proj,
        grad_w_fc,
        grad_w_out,
        jnp.stack([grad_gain_one, grad_gain_two]),
        jnp.stack([grad_offset_one, grad_offset_two]),
        grad_attn,
        jnp.stack([grad_bias_one, grad_bias_two]),
        grad_fc_bias,
    )
    return (grad_input, grads)


def store_slot(buffer, value, slot, valid):
    current = lax.dynamic_index_in_dim(buffer, slot, 0, keepdims=False)
    return lax.dynamic_update_index_in_dim(buffer, jnp.where(valid, value, current), slot, 0)


def shards(
    block_input,
    positions,
    cotangent,
    w_qkv,
    w_proj,
    w_fc,
    w_out,
    ln_gain,
    ln_bias,
    attn_bias,
    out_bias,
    fc_bias,
):
    section = lax.axis_index("section")
    ctx_index = lax.axis_index("ctx")
    local_seqs, local_rows, width = block_input.shape
    seq_len = positions.shape[1]
    micro = local_seqs // MB_SEQ
    gathered = (
        lax.all_gather(w_qkv, "fsdp", axis=1, tiled=True),
        lax.all_gather(w_proj, "fsdp", axis=1, tiled=True),
        lax.all_gather(w_fc, "fsdp", axis=1, tiled=True),
        lax.all_gather(w_out, "fsdp", axis=1, tiled=True),
        lax.all_gather(ln_gain, "fsdp", axis=2, tiled=True),
        lax.all_gather(ln_bias, "fsdp", axis=2, tiled=True),
        lax.all_gather(attn_bias, "fsdp", axis=2, tiled=True),
        lax.all_gather(out_bias, "fsdp", axis=2, tiled=True),
        lax.all_gather(fc_bias, "fsdp", axis=1, tiled=True),
    )
    resident = tuple((piece[0] for piece in gathered))
    inputs_split = block_input.reshape(micro, MB_SEQ, local_rows, width)
    cotan_split = cotangent.reshape(micro, MB_SEQ, local_rows, width)
    places_split = positions.reshape(micro, MB_SEQ, seq_len)
    kept_in = jnp.zeros((micro, MB_SEQ, local_rows, width), jnp.bfloat16)
    kept_mixed = jnp.zeros((micro, MB_SEQ, local_rows, width), jnp.bfloat16)
    kept_log = jnp.zeros((micro, MB_SEQ, H, local_rows), jnp.float32)
    outputs = jnp.zeros((micro, MB_SEQ, local_rows, width), jnp.bfloat16)
    arrived = jnp.zeros((MB_SEQ, local_rows, width), jnp.bfloat16)
    for tick in range(micro + 1):
        index = tick - section
        valid = (index >= 0) & (index < micro)
        slot = jnp.clip(index, 0, micro - 1)
        own_input = lax.dynamic_index_in_dim(inputs_split, slot, 0, keepdims=False)
        layer_in = jnp.where(section == 0, own_input, arrived)
        pos_seq = lax.dynamic_index_in_dim(places_split, slot, 0, keepdims=False)
        pos_query = lax.dynamic_slice_in_dim(pos_seq, ctx_index * local_rows, local_rows, 1)
        params = resident
        hidden = layer_in.astype(jnp.float32)
        normed, queries, key_rows, value_rows = front_half(params, hidden)
        mixed_full, log_total = attend_forward(queries, key_rows, value_rows, pos_seq, pos_query)
        mixed = mixed_full.astype(jnp.bfloat16)
        result = back_half(params, hidden, mixed)[4].astype(jnp.bfloat16)
        kept_in = store_slot(kept_in, layer_in, slot, valid)
        kept_mixed = store_slot(kept_mixed, mixed, slot, valid)
        kept_log = store_slot(kept_log, log_total, slot, valid)
        outputs = store_slot(outputs, result, slot, valid)
        arrived = shifted(result, "section", 1)
    grad_inputs = jnp.zeros((micro, MB_SEQ, local_rows, width), jnp.bfloat16)
    returned = jnp.zeros((MB_SEQ, local_rows, width), jnp.bfloat16)
    totals = None
    for tick in range(micro + 1):
        index = micro - 1 - tick + (1 - section)
        valid = (index >= 0) & (index < micro)
        slot = jnp.clip(index, 0, micro - 1)
        layer_in = lax.dynamic_index_in_dim(kept_in, slot, 0, keepdims=False)
        mixed = lax.dynamic_index_in_dim(kept_mixed, slot, 0, keepdims=False)
        log_total = lax.dynamic_index_in_dim(kept_log, slot, 0, keepdims=False)
        own_cotan = lax.dynamic_index_in_dim(cotan_split, slot, 0, keepdims=False)
        grad_out = jnp.where(section == 1, own_cotan, returned)
        pos_seq = lax.dynamic_index_in_dim(places_split, slot, 0, keepdims=False)
        pos_query = lax.dynamic_slice_in_dim(pos_seq, ctx_index * local_rows, local_rows, 1)
        params = resident
        grad_input, grads = layer_back(
            params, layer_in, mixed, log_total, grad_out, pos_seq, pos_query
        )
        gated = tuple((jnp.where(valid, term, 0.0) for term in grads))
        totals = (
            gated if totals is None else tuple((total + term for total, term in zip(totals, gated)))
        )
        grad_inputs = store_slot(grad_inputs, grad_input, slot, valid)
        returned = shifted(grad_input, "section", -1)
    whole = (
        lax.psum(totals[0].astype(jnp.bfloat16), "ctx").astype(jnp.float32),
        lax.psum(totals[1].astype(jnp.bfloat16), "ctx").astype(jnp.float32),
        lax.psum(totals[2].astype(jnp.bfloat16), "ctx").astype(jnp.float32),
        lax.psum(totals[3].astype(jnp.bfloat16), "ctx").astype(jnp.float32),
        lax.psum(totals[4].astype(jnp.bfloat16), "ctx").astype(jnp.float32),
        lax.psum(totals[5].astype(jnp.bfloat16), "ctx").astype(jnp.float32),
        lax.psum(totals[6].astype(jnp.bfloat16), "ctx").astype(jnp.float32),
        lax.psum(totals[7].astype(jnp.bfloat16), "ctx").astype(jnp.float32),
        lax.psum(totals[8].astype(jnp.bfloat16), "ctx").astype(jnp.float32),
    )
    shares = (
        lax.psum_scatter(
            whole[0].astype(jnp.bfloat16), "fsdp", scatter_dimension=0, tiled=True
        ).astype(jnp.float32),
        lax.psum_scatter(
            whole[1].astype(jnp.bfloat16), "fsdp", scatter_dimension=0, tiled=True
        ).astype(jnp.float32),
        lax.psum_scatter(
            whole[2].astype(jnp.bfloat16), "fsdp", scatter_dimension=0, tiled=True
        ).astype(jnp.float32),
        lax.psum_scatter(
            whole[3].astype(jnp.bfloat16), "fsdp", scatter_dimension=0, tiled=True
        ).astype(jnp.float32),
        lax.psum_scatter(
            whole[4].astype(jnp.bfloat16), "fsdp", scatter_dimension=1, tiled=True
        ).astype(jnp.float32),
        lax.psum_scatter(
            whole[5].astype(jnp.bfloat16), "fsdp", scatter_dimension=1, tiled=True
        ).astype(jnp.float32),
        lax.psum_scatter(
            whole[6].astype(jnp.bfloat16), "fsdp", scatter_dimension=1, tiled=True
        ).astype(jnp.float32),
        lax.psum_scatter(
            whole[7].astype(jnp.bfloat16), "fsdp", scatter_dimension=1, tiled=True
        ).astype(jnp.float32),
        lax.psum_scatter(
            whole[8].astype(jnp.bfloat16), "fsdp", scatter_dimension=0, tiled=True
        ).astype(jnp.float32),
    )
    section_out = outputs.reshape(local_seqs, local_rows, width)[None]
    section_in_grad = grad_inputs.reshape(local_seqs, local_rows, width)[None]
    return (
        section_out,
        section_in_grad,
        shares[0][None],
        shares[1][None],
        shares[2][None],
        shares[3][None],
        shares[4][None],
        shares[5][None],
        shares[6][None],
        shares[7][None],
        shares[8][None],
    )


def solution(mesh):
    return jax.shard_map(
        shards,
        mesh=mesh,
        in_specs=(
            P("fsdp", "ctx", None),
            P("fsdp", None),
            P("fsdp", "ctx", None),
            P("section", "fsdp", None),
            P("section", "fsdp", None),
            P("section", "fsdp", None),
            P("section", "fsdp", None),
            P("section", None, "fsdp"),
            P("section", None, "fsdp"),
            P("section", None, "fsdp"),
            P("section", None, "fsdp"),
            P("section", "fsdp"),
        ),
        out_specs=(
            P("section", "fsdp", "ctx", None),
            P("section", "fsdp", "ctx", None),
            P("section", "fsdp", None),
            P("section", "fsdp", None),
            P("section", "fsdp", None),
            P("section", "fsdp", None),
            P("section", None, "fsdp"),
            P("section", None, "fsdp"),
            P("section", None, "fsdp"),
            P("section", None, "fsdp"),
            P("section", "fsdp"),
        ),
        check_vma=False,
    )
```

profile of v0, /device:TPU:0, one launch (start us, length us, event | category | flops | bytes accessed | tf_op | source)
XLA Modules:
  0.0 2405.2 jit_solution(12556619019617481231)
XLA Ops:
  9.7 11.0 all_gather.76
  20.6 13.1 all_gather.75
  44.8 17.7 all-gather.21.cloned.1.call-done
  115.6 17.8 all-gather.25.cloned.1.call-done
  138.3 59.4 %all-gather.23.cloned.1.call-done = bf16[2,1024,768]{2,1,0:T(8,128)(2,1)} async-done(((bf16[2,256,768]{2,1,0:T(8,128)(2,1)}), bf16[2,1024,768]{2,1,0:T(8,128)(2,1)}) %all-gather.23.cloned.1.call-update) | async-done | bytes 3145744 | tf_op jit(solution)/shard_map/all_gather | solution.py:88
  202.4 14.9 fusion
  217.3 12.8 fusion.8
  230.2 13.9 broadcast_select_fusion
  248.1 36.6 %all-gather.31.cloned.1.call-done = bf16[1,3072,768]{2,1,0:T(8,128)(2,1)} async-done(((bf16[1,768,768]{2,1,0:T(8,128)(2,1)}), bf16[1,3072,768]{2,1,0:T(8,128)(2,1)}) %all-gather.31.cloned.1.call-update) | async-done | bytes 4718608 | tf_op jit(solution)/shard_map/all_gather | solution.py:255
  284.7 58.8 %all-gather.29.cloned.1.call-done = bf16[1,768,3072]{2,1,0:T(8,128)(2,1)} async-done(((bf16[1,192,3072]{2,1,0:T(8,128)(2,1)}), bf16[1,768,3072]{2,1,0:T(8,128)(2,1)}) %all-gather.29.cloned.1.call-update) | async-done | bytes 4718608 | tf_op jit(solution)/shard_map/all_gather | solution.py:254
  343.7 11.2 bitcast_dynamic-update-slice_fusion.8
  374.8 55.2 %all-gather.35.cloned.1.call-done = bf16[2,1024,768]{2,1,0:T(8,128)(2,1)} async-done(((bf16[2,256,768]{2,1,0:T(8,128)(2,1)}), bf16[2,1024,768]{2,1,0:T(8,128)(2,1)}) %all-gather.35.cloned.1.call-update) | async-done | bytes 3145744 | tf_op jit(solution)/shard_map/all_gather | solution.py:87
  435.2 14.9 fusion.1
  450.0 13.3 fusion.10
  463.3 31.0 %all-gather.33.cloned.1.call-done = bf16[2,1024,768]{2,1,0:T(8,128)(2,1)} async-done(((bf16[2,256,768]{2,1,0:T(8,128)(2,1)}), bf16[2,1024,768]{2,1,0:T(8,128)(2,1)}) %all-gather.33.cloned.1.call-update) | async-done | bytes 3145744 | tf_op jit(solution)/shard_map/all_gather | solution.py:88
  499.0 12.9 fusion.347
  515.0 11.6 bitcast_dynamic-update-slice_fusion.7
  547.8 52.9 %all-gather.39.cloned.1.call-done = bf16[2,1024,768]{2,1,0:T(8,128)(2,1)} async-done(((bf16[2,256,768]{2,1,0:T(8,128)(2,1)}), bf16[2,1024,768]{2,1,0:T(8,128)(2,1)}) %all-gather.39.cloned.1.call-update) | async-done | bytes 3145744 | tf_op jit(solution)/shard_map/all_gather | solution.py:87
  605.6 15.0 fusion.2
  621.9 13.3 fusion.12
  635.2 29.7 %all-gather.37.cloned.1.call-done = bf16[2,1024,768]{2,1,0:T(8,128)(2,1)} async-done(((bf16[2,256,768]{2,1,0:T(8,128)(2,1)}), bf16[2,1024,768]{2,1,0:T(8,128)(2,1)}) %all-gather.37.cloned.1.call-update) | async-done | bytes 3145744 | tf_op jit(solution)/shard_map/all_gather | solution.py:88
  669.6 13.2 fusion.346
  685.8 11.6 bitcast_dynamic-update-slice_fusion.6
  744.8 26.8 %all-gather.43.cloned.1.call-done = bf16[2,1024,768]{2,1,0:T(8,128)(2,1)} async-done(((bf16[2,256,768]{2,1,0:T(8,128)(2,1)}), bf16[2,1024,768]{2,1,0:T(8,128)(2,1)}) %all-gather.43.cloned.1.call-update) | async-done | bytes 3145744 | tf_op jit(solution)/shard_map/all_gather | solution.py:87
  776.3 15.0 fusion.3
  792.5 13.3 fusion.14
  805.8 30.0 %all-gather.41.cloned.1.call-done = bf16[2,1024,768]{2,1,0:T(8,128)(2,1)} async-done(((bf16[2,256,768]{2,1,0:T(8,128)(2,1)}), bf16[2,1024,768]{2,1,0:T(8,128)(2,1)}) %all-gather.41.cloned.1.call-update) | async-done | bytes 3145744 | tf_op jit(solution)/shard_map/all_gather | solution.py:88
  840.4 14.2 fusion.345
  886.8 12.7 all-gather.45.cloned.1.call-done
  907.1 14.3 fusion.671
  921.4 12.5 fusion.207
  943.8 19.3 all-gather.47.cloned.1.call-done
  967.8 17.9 multiply_convert_fusion.3
  1007.6 12.1 convert_reduce_fusion.27
  1022.0 92.6 %reduce-scatter.21.cloned.1.call-done = bf16[2,256,1536]{2,1,0:T(8,128)(2,1)} async-done(((bf16[2,1024,1536]{2,1,0:T(8,128)(2,1)}), bf16[2,256,1536]{2,1,0:T(8,128)(2,1)}) %reduce-scatter.21.cloned.1.call-update) | async-done | bytes 1572880 | tf_op jit(solution)/shard_map/reduce_scatter | solution.py:169
  1198.4 14.4 fusion.672
  1212.9 12.3 fusion.210
  1229.9 26.0 %all-gather.51.cloned.1.call-done = bf16[2,1024,768]{2,1,0:T(8,128)(2,1)} async-done(((bf16[2,256,768]{2,1,0:T(8,128)(2,1)}), bf16[2,1024,768]{2,1,0:T(8,128)(2,1)}) %all-gather.51.cloned.1.call-update) | async-done | bytes 3145744 | tf_op jit(solution)/shard_map/all_gather | solution.py:142
  1260.5 18.7 multiply_convert_fusion.2
  1315.3 11.0 convert_reduce_fusion.25
  1333.4 49.8 %all-gather.55.cloned.1.call-done = bf16[2,1024,768]{2,1,0:T(8,128)(2,1)} async-done(((bf16[2,256,768]{2,1,0:T(8,128)(2,1)}), bf16[2,1024,768]{2,1,0:T(8,128)(2,1)}) %all-gather.55.cloned.1.call-update) | async-done | bytes 3145744 | tf_op jit(solution)/shard_map/all_gather | solution.py:142
  1387.9 106.9 %reduce-scatter.23.cloned.1.call-done = bf16[2,256,1536]{2,1,0:T(8,128)(2,1)} async-done(((bf16[2,1024,1536]{2,1,0:T(8,128)(2,1)}), bf16[2,256,1536]{2,1,0:T(8,128)(2,1)}) %reduce-scatter.23.cloned.1.call-update) | async-done | bytes 1572880 | tf_op jit(solution)/shard_map/reduce_scatter | solution.py:169
  1505.4 10.6 fusion.673
  1537.7 12.9 fusion.213
  1560.4 18.1 multiply_convert_fusion.1
  1631.0 11.7 convert_reduce_fusion.23
  1645.0 90.9 %reduce-scatter.25.cloned.1.call-done = bf16[2,256,1536]{2,1,0:T(8,128)(2,1)} async-done(((bf16[2,1024,1536]{2,1,0:T(8,128)(2,1)}), bf16[2,256,1536]{2,1,0:T(8,128)(2,1)}) %reduce-scatter.25.cloned.1.call-update) | async-done | bytes 1572880 | tf_op jit(solution)/shard_map/reduce_scatter | solution.py:169
  1746.5 10.6 fusion.674
  1775.8 12.3 fusion.216
  1794.8 18.3 multiply_convert_fusion
  1861.7 13.9 fusion.45
  1876.3 10.5 fusion.184
  1886.8 10.2 fusion.185
  1903.3 14.2 fusion.41
  1948.9 11.5 fusion.49
  1997.8 38.6 %reduce-scatter.33.cloned.1.call-done = bf16[192,3072]{1,0:T(8,128)(2,1)} async-done(((bf16[768,3072]{1,0:T(8,128)(2,1)}), bf16[192,3072]{1,0:T(8,128)(2,1)}) %reduce-scatter.33.cloned.1.call-update) | async-done | bytes 1179664 | tf_op jit(solution)/shard_map/reduce_scatter | solution.py:332
  2036.3 60.0 %reduce-scatter.35.cloned.1.call-done = bf16[768,768]{1,0:T(8,128)(2,1)} async-done(((bf16[3072,768]{1,0:T(8,128)(2,1)}), bf16[768,768]{1,0:T(8,128)(2,1)}) %reduce-scatter.35.cloned.1.call-update) | async-done | bytes 1179664 | tf_op jit(solution)/shard_map/reduce_scatter | solution.py:335
  2096.3 50.4 %reduce-scatter.29.cloned.1.call-done = bf16[192,2304]{1,0:T(8,128)(2,1)} async-done(((bf16[768,2304]{1,0:T(8,128)(2,1)}), bf16[192,2304]{1,0:T(8,128)(2,1)}) %reduce-scatter.29.cloned.1.call-update) | async-done | bytes 884752 | tf_op jit(solution)/shard_map/reduce_scatter | solution.py:326
  2146.8 11.5 fusion.386
  2178.1 22.5 reduce-scatter.37.cloned.1.call-done
  2201.5 25.9 %reduce-scatter.39.cloned.1.call-done = bf16[192,2]{1,0:T(8,128)(2,1)} async-done(((bf16[768,2]{1,0:T(8,128)(2,1)}), bf16[192,2]{1,0:T(8,128)(2,1)}) %reduce-scatter.39.cloned.1.call-update) | async-done | bytes 784
  2228.3 25.9 %reduce-scatter.41.cloned.1.call-done = bf16[192,2]{1,0:T(8,128)(2,1)} async-done(((bf16[768,2]{1,0:T(8,128)(2,1)}), bf16[192,2]{1,0:T(8,128)(2,1)}) %reduce-scatter.41.cloned.1.call-update) | async-done | bytes 784
  2255.0 12.0 all-reduce.1
  2270.0 121.5 %all-reduce.5.cloned.1.call-done = (bf16[192,2304]{1,0:T(8,128)(2,1)}, bf16[192,768]{1,0:T(8,128)(2,1)}, bf16[192,3072]{1,0:T(8,128)(2,1)}, bf16[768,768]{1,0:T(8,128)(2,1)}) async-done(((bf16[192,2304]{1,0:T(8,128)(2,1)}, bf16[192,768]{1,0:T(8,128)(2,1)}, bf16[192,3072]{1,0:T(8,128)(2,1)}, bf16[768,768]{1,0:T(8,128)(2,1)}), (bf16[192,2304]{1,0:T(8,128)(2,1)}, bf16[192,768]{1,0:T(8,128)(2,1)}, ...) | async-done | bytes 3538960 | tf_op jit(solution)/shard_map/psum | solution.py:315
  (972 shorter events, 711.1 us)
Async XLA Ops:
  7.2 27.9 %copy-start.26 = (bf16[6,256,768]{2,1,0:T(8,128)(2,1)S(1)}, bf16[6,256,768]{2,1,0:T(8,128)(2,1)}, u32[]{:S(2)}) copy-start(bf16[6,256,768]{2,1,0:T(8,128)(2,1)} %param.12) | copy-start | bytes 7077892
  7.2 55.3 %all-gather.21.cloned.1.call-start = ((), (), s32[]{:S(2)}) async-start(), calls=%async_computation.12 | async-start | bytes 4423680 | tf_op jit(solution)/shard_map/all_gather | solution.py:252
  7.9 125.5 %all-gather.25.cloned.1.call-start = ((), (), s32[]{:S(2)}) async-start(), calls=%async_computation.14 | async-start | bytes 3932160 | tf_op jit(solution)/shard_map/all_gather | solution.py:87
  40.1 303.5 %copy-start.187 = (f32[768]{0:T(1024)}, f32[768]{0:T(1024)S(1)}, u32[]{:S(2)}) copy-start(f32[768]{0:T(1024)S(1)} %get-tuple-element.48) | copy-start | bytes 9220
  40.1 1093.8 %copy-start.93 = (f32[768]{0:T(1024)}, f32[768]{0:T(1024)S(1)}, u32[]{:S(2)}) copy-start(f32[768]{0:T(1024)S(1)} %get-tuple-element.49) | copy-start | bytes 9220
  44.8 298.9 %copy-start.131 = (f32[768]{0:T(1024)}, f32[768]{0:T(1024)S(1)}, u32[]{:S(2)}) copy-start(f32[768]{0:T(1024)S(1)} %get-tuple-element.46) | copy-start | bytes 9220
  44.8 1698.1 %copy-start.88 = (f32[768]{0:T(1024)}, f32[768]{0:T(1024)S(1)}, u32[]{:S(2)}) copy-start(f32[768]{0:T(1024)S(1)} %get-tuple-element.47) | copy-start | bytes 9220
  69.8 128.0 %all-gather.23.cloned.1.call-start = ((), (), s32[]{:S(2)}) async-start(), calls=%async_computation.13 | async-start | bytes 3932160 | tf_op jit(solution)/shard_map/all_gather | solution.py:88
  84.7 453.4 %copy-start.128 = (f32[768]{0:T(1024)}, f32[768]{0:T(1024)S(1)}, u32[]{:S(2)}) copy-start(f32[768]{0:T(1024)S(1)} %get-tuple-element.53) | copy-start | bytes 9220
  84.7 629.0 %copy-start.126 = (f32[768]{0:T(1024)}, f32[768]{0:T(1024)S(1)}, u32[]{:S(2)}) copy-start(f32[768]{0:T(1024)S(1)} %get-tuple-element.52) | copy-start | bytes 9220
  88.1 156.1 %all-gather.27.cloned.1.call-start = ((), (), s32[]{:S(2)}) async-start(), calls=%async_computation.15 | async-start | bytes 1474560 | tf_op jit(solution)/shard_map/all_gather | solution.py:253
  88.6 196.1 %all-gather.31.cloned.1.call-start = ((), (), s32[]{:S(2)}) async-start(), calls=%async_computation.17 | async-start | bytes 5898240 | tf_op jit(solution)/shard_map/all_gather | solution.py:255
  89.2 254.3 %all-gather.29.cloned.1.call-start = ((), (), s32[]{:S(2)}) async-start(), calls=%async_computation.16 | async-start | bytes 5898240 | tf_op jit(solution)/shard_map/all_gather | solution.py:254
  89.8 340.2 %all-gather.35.cloned.1.call-start = ((), (), s32[]{:S(2)}) async-start(), calls=%async_computation.19 | async-start | bytes 3932160 | tf_op jit(solution)/shard_map/all_gather | solution.py:87
  97.3 246.3 %copy-start.208 = (f32[1,3072]{1,0:T(1,128)}, f32[1,3072]{1,0:T(1,128)S(1)}, u32[]{:S(2)}) copy-start(f32[1,3072]{1,0:T(1,128)S(1)} %convert_element_type.812) | copy-start | bytes 36868
  112.7 131.4 %copy-start.230 = (f32[768]{0:T(1024)}, f32[768]{0:T(1024)S(1)}, u32[]{:S(2)}) copy-start(f32[768]{0:T(1024)S(1)} %get-tuple-element.51) | copy-start | bytes 9220
  112.8 230.9 %copy-start.228 = (f32[768]{0:T(1024)}, f32[768]{0:T(1024)S(1)}, u32[]{:S(2)}) copy-start(f32[768]{0:T(1024)S(1)} %get-tuple-element.50) | copy-start | bytes 9220
  113.1 117.0 %copy-start.62 = (pred[2,256,1024]{2,1,0:T(8,128)(4,1)}, pred[2,256,1024]{2,1,0:T(8,128)(4,1)S(1)}, u32[]{:S(2)}) copy-start(pred[2,256,1024]{2,1,0:T(8,128)(4,1)S(1)} %broadcast_compare_fusion.3) | copy-start | bytes 1572868
  354.9 3.8 collective-permute-start
  366.4 127.9 %all-gather.33.cloned.1.call-start = ((), (), s32[]{:S(2)}) async-start(), calls=%async_computation.18 | async-start | bytes 3932160 | tf_op jit(solution)/shard_map/all_gather | solution.py:88
  369.7 231.0 %all-gather.39.cloned.1.call-start = ((), (), s32[]{:S(2)}) async-start(), calls=%async_computation.21 | async-start | bytes 3932160 | tf_op jit(solution)/shard_map/all_gather | solution.py:87
  370.2 79.9 %copy-start.64 = (pred[2,256,1024]{2,1,0:T(8,128)(4,1)}, pred[2,256,1024]{2,1,0:T(8,128)(4,1)S(1)}, u32[]{:S(2)}) copy-start(pred[2,256,1024]{2,1,0:T(8,128)(4,1)S(1)} %broadcast_compare_fusion.2) | copy-start | bytes 1572868
  526.6 4.0 collective-permute-start.1
  538.1 126.8 %all-gather.37.cloned.1.call-start = ((), (), s32[]{:S(2)}) async-start(), calls=%async_computation.20 | async-start | bytes 3932160 | tf_op jit(solution)/shard_map/all_gather | solution.py:88
  541.4 230.2 %all-gather.43.cloned.1.call-start = ((), (), s32[]{:S(2)}) async-start(), calls=%async_computation.23 | async-start | bytes 3932160 | tf_op jit(solution)/shard_map/all_gather | solution.py:87
  697.4 4.0 collective-permute-start.2
  702.9 1040.0 %copy-start = (bf16[3,2,256,768]{3,2,1,0:T(8,128)(2,1)}, bf16[3,2,256,768]{3,2,1,0:T(8,128)(2,1)S(1)}, u32[]{:S(2)}) copy-start(bf16[3,2,256,768]{3,2,1,0:T(8,128)(2,1)S(1)} %get-tuple-element.91) | copy-start | bytes 7077892
  708.9 126.8 %all-gather.41.cloned.1.call-start = ((), (), s32[]{:S(2)}) async-start(), calls=%async_computation.22 | async-start | bytes 3932160 | tf_op jit(solution)/shard_map/all_gather | solution.py:88
  710.0 435.3 %copy-start.109 = (f32[2,256]{1,0:T(2,128)}, f32[2,256]{1,0:T(2,128)S(1)}, u32[]{:S(2)}) copy-start(f32[2,256]{1,0:T(2,128)S(1)} %broadcast_multiply_fusion.6) | copy-start | bytes 6148
  717.0 182.5 %all-gather.45.cloned.1.call-start = ((), (), s32[]{:S(2)}) async-start(), calls=%async_computation.24 | async-start | bytes 3932160 | tf_op jit(solution)/shard_map/all_gather | solution.py:141
  719.6 243.5 %all-gather.47.cloned.1.call-start = ((), (), s32[]{:S(2)}) async-start(), calls=%async_computation.25 | async-start | bytes 3932160 | tf_op jit(solution)/shard_map/all_gather | solution.py:142
  744.6 370.1 %reduce-scatter.21.cloned.1.call-start = ((), (), s32[]{:S(2)}) async-start(), calls=%async_computation.26 | async-start | bytes 7864320 | tf_op jit(solution)/shard_map/reduce_scatter | solution.py:169
  1005.0 188.7 %all-gather.49.cloned.1.call-start = ((), (), s32[]{:S(2)}) async-start(), calls=%async_computation.27 | async-start | bytes 3932160 | tf_op jit(solution)/shard_map/all_gather | solution.py:141
  1007.6 126.3 %copy-start.111 = (f32[2,256]{1,0:T(2,128)}, f32[2,256]{1,0:T(2,128)S(1)}, u32[]{:S(2)}) copy-start(f32[2,256]{1,0:T(2,128)S(1)} %get-tuple-element.201) | copy-start | bytes 6148
  1128.1 127.8 %all-gather.51.cloned.1.call-start = ((), (), s32[]{:S(2)}) async-start(), calls=%async_computation.28 | async-start | bytes 3932160 | tf_op jit(solution)/shard_map/all_gather | solution.py:142
  1139.8 188.9 %all-gather.53.cloned.1.call-start = ((), (), s32[]{:S(2)}) async-start(), calls=%async_computation.30 | async-start | bytes 3932160 | tf_op jit(solution)/shard_map/all_gather | solution.py:141
  1142.7 240.6 %all-gather.55.cloned.1.call-start = ((), (), s32[]{:S(2)}) async-start(), calls=%async_computation.31 | async-start | bytes 3932160 | tf_op jit(solution)/shard_map/all_gather | solution.py:142
  1151.5 10.8 collective-permute-start.3
  1162.3 332.6 %reduce-scatter.23.cloned.1.call-start = ((), (), s32[]{:S(2)}) async-start(), calls=%async_computation.29 | async-start | bytes 7864320 | tf_op jit(solution)/shard_map/reduce_scatter | solution.py:169
  1298.7 312.6 %all-gather.57.cloned.1.call-start = ((), (), s32[]{:S(2)}) async-start(), calls=%async_computation.33 | async-start | bytes 3932160 | tf_op jit(solution)/shard_map/all_gather | solution.py:141
  1301.2 323.0 %all-gather.59.cloned.1.call-start = ((), (), s32[]{:S(2)}) async-start(), calls=%async_computation.34 | async-start | bytes 3932160 | tf_op jit(solution)/shard_map/all_gather | solution.py:142
  1315.3 420.7 %reduce-scatter.25.cloned.1.call-start = ((), (), s32[]{:S(2)}) async-start(), calls=%async_computation.32 | async-start | bytes 7864320 | tf_op jit(solution)/shard_map/reduce_scatter | solution.py:169
  1333.4 161.4 %copy-start.115 = (f32[2,256]{1,0:T(2,128)S(1)}, f32[2,256]{1,0:T(2,128)}, u32[]{:S(2)}) copy-start(f32[2,256]{1,0:T(2,128)} %broadcast_multiply_fusion.4) | copy-start | bytes 6148
  1387.9 112.5 %copy-start.121 = (f32[2,256]{1,0:T(2,128)S(1)}, f32[2,256]{1,0:T(2,128)}, u32[]{:S(2)}) copy-start(f32[2,256]{1,0:T(2,128)} %copy-done.120) | copy-start | bytes 6148
  1503.8 12.2 collective-permute-start.4
  1598.0 350.9 %reduce-scatter.27.cloned.1.call-start = ((), (), s32[]{:S(2)}) async-start(), calls=%async_computation.35 | async-start | bytes 7864320 | tf_op jit(solution)/shard_map/reduce_scatter | solution.py:169
  1631.0 105.0 %copy-start.112 = (f32[2,256]{1,0:T(2,128)S(1)}, f32[2,256]{1,0:T(2,128)}, u32[]{:S(2)}) copy-start(f32[2,256]{1,0:T(2,128)} %copy-done.111) | copy-start | bytes 6148
  1645.0 96.5 %copy-start.124 = (f32[2,256]{1,0:T(2,128)S(1)}, f32[2,256]{1,0:T(2,128)}, u32[]{:S(2)}) copy-start(f32[2,256]{1,0:T(2,128)} %copy-done.123) | copy-start | bytes 6148
  1744.9 12.2 collective-permute-start.5
  1832.2 165.6 %reduce-scatter.31.cloned.1.call-start = ((), (), s32[]{:S(2)}) async-start(), calls=%async_computation.37 | async-start | bytes 1474560 | tf_op jit(solution)/shard_map/reduce_scatter | solution.py:329
  1852.6 183.7 %reduce-scatter.33.cloned.1.call-start = ((), (), s32[]{:S(2)}) async-start(), calls=%async_computation.38 | async-start | bytes 5898240 | tf_op jit(solution)/shard_map/reduce_scatter | solution.py:332
  1875.7 220.6 %reduce-scatter.35.cloned.1.call-start = ((), (), s32[]{:S(2)}) async-start(), calls=%async_computation.39 | async-start | bytes 5898240 | tf_op jit(solution)/shard_map/reduce_scatter | solution.py:335
  1917.6 229.1 %reduce-scatter.29.cloned.1.call-start = ((), (), s32[]{:S(2)}) async-start(), calls=%async_computation.36 | async-start | bytes 4423680 | tf_op jit(solution)/shard_map/reduce_scatter | solution.py:326
  1960.5 212.9 %reduce-scatter.43.cloned.1.call-start = ((), (), s32[]{:S(2)}) async-start(), calls=%async_computation.43 | async-start | bytes 245760
  1984.3 216.3 %reduce-scatter.37.cloned.1.call-start = ((), (), s32[]{:S(2)}) async-start(), calls=%async_computation.40 | async-start | bytes 245760
  1992.7 234.7 %reduce-scatter.39.cloned.1.call-start = ((), (), s32[]{:S(2)}) async-start(), calls=%async_computation.41 | async-start | bytes 245760
  1995.0 259.2 %reduce-scatter.41.cloned.1.call-start = ((), (), s32[]{:S(2)}) async-start(), calls=%async_computation.42 | async-start | bytes 245760
  1995.9 395.6 %all-reduce.5.cloned.1.call-start = ((), (), s32[]{:S(2)}) async-start(), calls=%async_computation.44 | async-start | bytes 7077888 | tf_op jit(solution)/shard_map/psum | solution.py:315
  1996.0 150.7 %copy-start.135 = (f32[768]{0:T(1024)S(1)}, f32[768]{0:T(1024)}, u32[]{:S(2)}) copy-start(f32[768]{0:T(1024)} %copy-done.131) | copy-start | bytes 9220
  1996.0 150.7 %copy-start.194 = (f32[768]{0:T(1024)S(1)}, f32[768]{0:T(1024)}, u32[]{:S(2)}) copy-start(f32[768]{0:T(1024)} %copy-done.187) | copy-start | bytes 9220
  1996.0 150.7 %copy-start.214 = (f32[1,3072]{1,0:T(1,128)S(1)}, f32[1,3072]{1,0:T(1,128)}, u32[]{:S(2)}) copy-start(f32[1,3072]{1,0:T(1,128)} %copy-done.208) | copy-start | bytes 36868
  1996.0 150.7 %copy-start.229 = (f32[768]{0:T(1024)S(1)}, f32[768]{0:T(1024)}, u32[]{:S(2)}) copy-start(f32[768]{0:T(1024)} %copy-done.228) | copy-start | bytes 9220
  2146.8 27.5 %copy-start.46 = (bf16[2,256,768]{2,1,0:T(8,128)(2,1)S(1)}, bf16[2,256,768]{2,1,0:T(8,128)(2,1)}, u32[]{:S(2)}) copy-start(bf16[2,256,768]{2,1,0:T(8,128)(2,1)} %copy-done.44) | copy-start | bytes 2359300
  2146.8 27.5 %copy-start.182 = (f32[2,256]{1,0:T(2,128)S(1)}, f32[2,256]{1,0:T(2,128)}, u32[]{:S(2)}) copy-start(f32[2,256]{1,0:T(2,128)} %copy-done.181) | copy-start | bytes 6148
  (254 other events, 1555.7 us)
Sparse Core Ops, SparseCore 0:
  9.9 52.5 all-gather.20
  69.9 63.4 all-gather.24
  135.6 62.1 all-gather.22
  199.5 26.4 all-gather.26
  227.6 57.0 all-gather.30
  286.4 57.0 all-gather.28
  366.5 63.4 all-gather.34
  432.2 62.1 all-gather.32
  538.2 62.5 all-gather.38
  602.7 62.1 all-gather.36
  709.0 62.5 all-gather.42
  773.6 62.1 all-gather.40
  837.3 62.1 all-gather.44
  900.9 62.1 all-gather.46
  1005.2 109.4 reduce-scatter.20
  1128.2 63.9 all-gather.48
  1193.7 62.1 all-gather.50
  1257.3 62.1 all-gather.52
  1321.0 62.1 all-gather.54
  1385.4 109.4 reduce-scatter.22
  1496.4 63.9 all-gather.56
  1562.0 62.1 all-gather.58
  1626.5 109.4 reduce-scatter.24
  1832.3 111.9 reduce-scatter.26
  1947.2 29.0 reduce-scatter.30
  1979.2 57.0 reduce-scatter.32
  2039.1 57.0 reduce-scatter.34
  2099.4 47.2 reduce-scatter.28
  2149.4 23.9 reduce-scatter.42
  2176.6 23.9 reduce-scatter.36
  2203.4 23.9 reduce-scatter.38
  2230.2 23.9 reduce-scatter.40
  2256.7 134.7 all-reduce.4
where the time goes:
time: 2420 us; the launch traced here: 2410 us
  waiting for transfers between devices  1180 us (49%)
  matrix products  668 us (28%)
  local copies, waits for them, and re-layouts  264 us (11%)
  other arithmetic  192 us (8%)
  blocking collectives  71.8 us (3%)
    reduce_scatter x4, waiting for transfers between devices, attend_back(): lax.psum_scatter(joined.astype(jnp.bfloat16), 'ctx', scatter_dimension=1,...  290 us
    all_gather x4, waiting for transfers between devices, attend_forward(): key_piece = lax.all_gather(key_rows, 'ctx', axis=1, tiled=True)  153 us
    all_gather x4, waiting for transfers between devices, attend_forward(): value_piece = lax.all_gather(value_rows, 'ctx', axis=1, tiled=True)  150 us
    psum x1, waiting for transfers between devices, shards(): lax.psum(totals[0].astype(jnp.bfloat16), 'ctx').astype(jnp.float32)  122 us
    dot_general x16, matrix products, outer_sum(): jnp.einsum('td,te->de', flatten(left), flatten(right), preferred_element_...  110 us
    dot_general x24, matrix products, project_rows(): jnp.einsum('bsd,de->bse', rows, matrix, preferred_element_type=jnp.float32)  109 us
    all_gather x4, waiting for transfers between devices, attend_back(): value_piece = lax.all_gather(value_rows, 'ctx', axis=1, tiled=True)  103 us
    dot_general x16, matrix products, project_back(): jnp.einsum('bse,de->bsd', grads, matrix, preferred_element_type=jnp.float32)  82 us
  transfers between devices with their start and end apart: 39, of which 30 were waited for; matrix products, arithmetic and copies ran while one was open for 35% of the time, Pallas kernels for 0%

commit v1 on v0

v1 whole, which is shorter than its diff:
```python
import functools

import jax
import jax.numpy as jnp
from jax import lax
from jax.experimental import pallas as pl
from jax.experimental.pallas import tpu as pltpu
from jax.sharding import PartitionSpec as P

H = 12
HD = 64
PAIR = 2 * HD
SCALE = HD**-0.5

masked_score = -1e30
norm_eps = 1e-05
f32 = jnp.float32
bf16 = jnp.bfloat16


def layer_norm(hidden, gain, offset):
    center = hidden - jnp.mean(hidden, axis=-1, keepdims=True)
    spread = jnp.mean(center * center, axis=-1, keepdims=True)
    return center * lax.rsqrt(spread + norm_eps) * gain + offset


def gelu_tanh(inputs):
    return jax.nn.gelu(inputs, approximate=True)


def mm(left, right):
    return lax.dot_general(left, right, (((1,), (0,)), ((), ())), preferred_element_type=f32)


def mm_nt(left, right):
    return lax.dot_general(left, right, (((1,), (1,)), ((), ())), preferred_element_type=f32)


def mm_tn(left, right):
    return lax.dot_general(left, right, (((0,), (0,)), ((), ())), preferred_element_type=f32)


def masked_scores(keys, queries, start, block):
    scores = mm_nt(keys, queries)
    down = lax.broadcasted_iota(jnp.int32, (block, block), 0)
    across = lax.broadcasted_iota(jnp.int32, (block, block), 1)
    corner = jnp.where(across >= down, scores[start:], masked_score)
    if start == 0:
        return corner
    return jnp.concatenate([scores[:start], corner], axis=0)


def attend_kernel(block, q_ref, k_ref, v_ref, o_ref, log_ref):
    length = q_ref.shape[0]
    for head in range(2):
        cols = slice(head * HD, (head + 1) * HD)
        for start in range(0, length, block):
            end = start + block
            queries = (q_ref[start:end, cols].astype(f32) * SCALE).astype(bf16)
            scores = masked_scores(k_ref[:end, cols], queries, start, block)
            top = jnp.max(scores, axis=0, keepdims=True)
            weights = jnp.exp(scores - top)
            total = jnp.sum(weights, axis=0, keepdims=True)
            mixed = mm_tn(v_ref[:end, cols], weights.astype(bf16)) / total
            o_ref[start:end, cols] = mixed.T.astype(bf16)
            log_ref[0, 0, head : head + 1, start:end] = top + jnp.log(total)


def attend_back_kernel(
    block, q_ref, k_ref, v_ref, do_ref, o_ref, log_ref, dq_ref, dk_ref, dv_ref, dk_sum, dv_sum
):
    length = q_ref.shape[0]
    for head in range(2):
        cols = slice(head * HD, (head + 1) * HD)
        for start in range(length - block, -1, -block):
            end = start + block
            queries = (q_ref[start:end, cols].astype(f32) * SCALE).astype(bf16)
            grads = do_ref[start:end, cols]
            product = grads.astype(f32) * o_ref[start:end, cols].astype(f32)
            delta = jnp.sum(product.T, axis=0, keepdims=True)
            keys = k_ref[:end, cols]
            scores = masked_scores(keys, queries, start, block)
            probs = jnp.exp(scores - log_ref[0, 0, head : head + 1, start:end])
            grad_probs = mm_nt(v_ref[:end, cols], grads)
            grad_scores = (probs * (grad_probs - delta)).astype(bf16)
            dv = mm(probs.astype(bf16), grads)
            dk = mm(grad_scores, queries)
            if end == length:
                dv_sum[:end, cols] = dv
                dk_sum[:end, cols] = dk
            else:
                dv_sum[:end, cols] += dv
                dk_sum[:end, cols] += dk
            dq = mm_tn(keys, grad_scores) * SCALE
            dq_ref[start:end, cols] = dq.T.astype(bf16)
    dk_ref[...] = dk_sum[...].astype(bf16)
    dv_ref[...] = dv_sum[...].astype(bf16)


def query_block(length):
    return 256 if length % 256 == 0 else length


def head_spec(length, offset):
    return pl.BlockSpec((length, PAIR), lambda b, h: (b, offset + h))


def log_spec(length):
    return pl.BlockSpec((1, 1, 2, length), lambda b, h: (b, h, 0, 0))


def attend_forward(project, length):
    rows = project.shape[0]
    count = rows // length
    pairs = H // 2
    return pl.pallas_call(
        functools.partial(attend_kernel, query_block(length)),
        grid=(count, pairs),
        in_specs=[head_spec(length, 0), head_spec(length, pairs), head_spec(length, 2 * pairs)],
        out_specs=[head_spec(length, 0), log_spec(length)],
        out_shape=[
            jax.ShapeDtypeStruct((rows, H * HD), bf16),
            jax.ShapeDtypeStruct((count, pairs, 2, length), f32),
        ],
        compiler_params=pltpu.CompilerParams(vmem_limit_bytes=40 * 1024 * 1024),
        cost_estimate=pl.CostEstimate(
            flops=8 * rows * length * H * HD,
            bytes_accessed=8 * rows * H * HD,
            transcendentals=rows * length * H // 2,
        ),
    )(project, project, project)


def attend_back(project, grad_mixed, mixed, log_total, length):
    rows = project.shape[0]
    count = rows // length
    pairs = H // 2
    return pl.pallas_call(
        functools.partial(attend_back_kernel, query_block(length)),
        grid=(count, pairs),
        in_specs=[
            head_spec(length, 0),
            head_spec(length, pairs),
            head_spec(length, 2 * pairs),
            head_spec(length, 0),
            head_spec(length, 0),
            log_spec(length),
        ],
        out_specs=[head_spec(length, 0)] * 3,
        out_shape=[jax.ShapeDtypeStruct((rows, H * HD), bf16)] * 3,
        scratch_shapes=[pltpu.VMEM((length, PAIR), f32)] * 2,
        compiler_params=pltpu.CompilerParams(vmem_limit_bytes=40 * 1024 * 1024),
        cost_estimate=pl.CostEstimate(
            flops=20 * rows * length * H * HD,
            bytes_accessed=16 * rows * H * HD,
            transcendentals=rows * length * H // 2,
        ),
    )(project, project, project, grad_mixed, mixed, log_total)


def layer_forward(weights, smalls, layer_in, length):
    w_qkv, w_proj, w_fc, w_out = weights
    gains, offsets, attn_bias, out_bias, fc_bias = smalls
    hidden = layer_in.astype(f32)
    width = hidden.shape[-1]
    normed = layer_norm(hidden, gains[0], offsets[0]).astype(bf16)
    bias = jnp.concatenate([attn_bias[0], jnp.zeros((width,), f32), attn_bias[1]])
    project = (mm(normed, w_qkv) + bias).astype(bf16)
    mixed, log_total = attend_forward(project, length)
    after = hidden + mm(mixed, w_proj) + out_bias[0]
    normed_two = layer_norm(after, gains[1], offsets[1]).astype(bf16)
    inner = mm(normed_two, w_fc) + fc_bias
    active = gelu_tanh(inner).astype(bf16)
    result = (after + mm(active, w_out) + out_bias[1]).astype(bf16)
    return result, (layer_in, normed, project, mixed, log_total, after, normed_two, inner, active)


def row_sum(rows):
    return jnp.sum(rows.astype(f32), axis=0)


def layer_back(weights, smalls, kept, grad_out, length, send):
    w_qkv, w_proj, w_fc, w_out = weights
    gains, offsets, attn_bias, out_bias, fc_bias = smalls
    layer_in, normed, project, mixed, log_total, after, normed_two, inner, active = kept
    grad_w_out = send(mm_tn(active, grad_out).astype(bf16))
    grad_bias_two = row_sum(grad_out)
    grad_active = mm_nt(grad_out, w_out)
    _, gelu_pull = jax.vjp(gelu_tanh, inner)
    grad_inner = gelu_pull(grad_active)[0].astype(bf16)
    grad_w_fc = send(mm_tn(normed_two, grad_inner).astype(bf16))
    grad_fc_bias = row_sum(grad_inner)
    grad_normed_two = mm_nt(grad_inner, w_fc)
    _, norm_pull = jax.vjp(layer_norm, after, gains[1], offsets[1])
    grad_after, grad_gain_two, grad_offset_two = norm_pull(grad_normed_two)
    grad_after = grad_after + grad_out.astype(f32)
    grad_branch = grad_after.astype(bf16)
    grad_w_proj = send(mm_tn(mixed, grad_branch).astype(bf16))
    grad_bias_one = row_sum(grad_branch)
    grad_mixed = mm_nt(grad_branch, w_proj).astype(bf16)
    grad_q, grad_k, grad_v = attend_back(project, grad_mixed, mixed, log_total, length)
    grad_project = jnp.concatenate([grad_q, grad_k, grad_v], axis=-1)
    grad_w_qkv = send(mm_tn(normed, grad_project).astype(bf16))
    grad_normed = mm_nt(grad_project, w_qkv)
    _, first_pull = jax.vjp(layer_norm, layer_in.astype(f32), gains[0], offsets[0])
    grad_hidden, grad_gain_one, grad_offset_one = first_pull(grad_normed)
    grad_input = (grad_after + grad_hidden).astype(bf16)
    small = (
        jnp.stack(
            [
                grad_gain_one,
                grad_gain_two,
                grad_offset_one,
                grad_offset_two,
                row_sum(grad_q),
                row_sum(grad_v),
                grad_bias_one,
                grad_bias_two,
            ]
        ),
        grad_fc_bias,
    )
    return grad_input, (grad_w_qkv, grad_w_proj, grad_w_fc, grad_w_out), small


def swap(value):
    return lax.ppermute(value, "section", [(0, 1), (1, 0)])


def shards(
    block_input,
    positions,
    cotangent,
    w_qkv,
    w_proj,
    w_fc,
    w_out,
    ln_gain,
    ln_bias,
    attn_bias,
    out_bias,
    fc_bias,
):
    section = lax.axis_index("section")
    ctx_index = lax.axis_index("ctx")
    first = section == 0
    sections = lax.axis_size("section")
    ctxs = lax.axis_size("ctx")
    fsdps = lax.axis_size("fsdp")
    local_seqs, local_rows, width = block_input.shape
    length = positions.shape[1]
    per = -(-local_seqs // (sections * ctxs))
    slots = sections * ctxs * per
    spare = slots - local_seqs
    shard_width = ln_gain.shape[2]

    def trade(value):
        other = swap(value)
        return jnp.where(first, value, other), jnp.where(first, other, value)

    pack = jnp.concatenate(
        [ln_gain[0], ln_bias[0], attn_bias[0], out_bias[0], fc_bias[0].reshape(-1, shard_width)]
    )
    pack = lax.all_gather(pack, "fsdp", axis=0)
    packs = trade(pack)

    def unpack(packed):
        vectors = jnp.transpose(packed[:, :8], (1, 0, 2)).reshape(8, -1).astype(f32)
        fc = packed[:, 8:].reshape(-1).astype(f32)
        return vectors[0:2], vectors[2:4], vectors[4:6], vectors[6:8], fc

    smalls = [unpack(packed) for packed in packs]

    def halves(matrix):
        rows = matrix.shape[0] // 2
        low, high = matrix[:rows], matrix[rows:]
        arrived = swap(jnp.where(first, high, low))
        mine = jnp.where(first, low, high)
        return jnp.where(first, mine, arrived), jnp.where(first, arrived, mine)

    pieces = [halves(matrix[0]) for matrix in (w_qkv, w_proj, w_fc, w_out)]

    def whole_weight(piece):
        gathered = lax.all_gather(piece, "fsdp", axis=0)
        low, high = trade(gathered)
        return jnp.stack([low, high], axis=1).reshape(-1, piece.shape[-1])

    weights = [tuple(whole_weight(piece[layer]) for piece in pieces) for layer in range(2)]

    def own(padded):
        return lax.dynamic_slice_in_dim(padded, section * (ctxs * per), ctxs * per, 0)

    def bring(rows):
        padded = jnp.pad(rows, ((0, spare), (0, 0), (0, 0)))
        mine = own(padded).reshape(ctxs, per, local_rows, width)
        moved = lax.all_to_all(mine, "ctx", 0, 0, tiled=True)
        return jnp.transpose(moved, (1, 0, 2, 3)).reshape(per, length, width)

    places = own(jnp.pad(positions, ((0, spare), (0, 0)))).reshape(ctxs, per, length)
    places = lax.dynamic_index_in_dim(places, ctx_index, 0, keepdims=False)
    order = (
        lax.broadcasted_iota(jnp.int32, (per, length, length), 1) == places[:, None, :]
    ).astype(bf16)

    def to_sorted(rows):
        return (
            jnp.einsum("bpt,btd->bpd", order, rows, preferred_element_type=f32)
            .astype(bf16)
            .reshape(per * length, width)
        )

    def to_stored(rows):
        return jnp.einsum(
            "bpt,bpd->btd", order, rows.reshape(per, length, width), preferred_element_type=f32
        ).astype(bf16)

    def home(zero, one):
        arrived = swap(jnp.where(first, one, zero))
        mine = jnp.where(first, zero, one)
        both = jnp.stack([jnp.where(first, mine, arrived), jnp.where(first, arrived, mine)])
        both = both.reshape(sections, per, ctxs, local_rows, width)
        moved = lax.all_to_all(both, "ctx", 2, 2, tiled=True)
        ordered = jnp.transpose(moved, (0, 2, 1, 3, 4)).reshape(slots, local_rows, width)
        return ordered[:local_seqs][None]

    start = to_sorted(bring(block_input))
    grad_final = to_sorted(bring(cotangent))
    middle, kept_zero = layer_forward(weights[0], smalls[0], start, length)
    final, kept_one = layer_forward(weights[1], smalls[1], middle, length)
    section_out = home(to_stored(middle), to_stored(final))

    def send(grad):
        cut = grad.reshape(fsdps, 2, -1, grad.shape[-1])
        low, high = cut[:, 0], cut[:, 1]
        arrived = swap(jnp.where(first, high, low))
        mine = jnp.where(first, low, high)
        both = (mine.astype(f32) + arrived.astype(f32)).astype(bf16)
        scattered = lax.psum_scatter(both, "fsdp", scatter_dimension=0, tiled=False)
        return lax.psum(scattered, "ctx")

    grad_middle, grads_one, small_one = layer_back(
        weights[1], smalls[1], kept_one, grad_final, length, send
    )
    grad_start, grads_zero, small_zero = layer_back(
        weights[0], smalls[0], kept_zero, grad_middle, length, send
    )
    section_in_grad = home(to_stored(grad_start), to_stored(grad_middle))

    def finish(zero, one):
        arrived = swap(jnp.where(first, one, zero))
        mine = jnp.where(first, zero, one)
        low = jnp.where(first, mine, arrived)
        high = jnp.where(first, arrived, mine)
        return jnp.concatenate([low, high], axis=0).astype(f32)[None]

    big = [finish(zero, one) for zero, one in zip(grads_zero, grads_one)]

    def repack(small):
        vectors, fc = small
        vectors = jnp.transpose(vectors.reshape(8, fsdps, shard_width), (1, 0, 2))
        return jnp.concatenate([vectors, fc.reshape(fsdps, -1, shard_width)], axis=1)

    packed = jnp.stack([repack(small_zero), repack(small_one)])
    packed = lax.psum(packed, ("section", "ctx", "fsdp"))
    packed = lax.dynamic_index_in_dim(packed, section, 0, keepdims=False)
    packed = lax.dynamic_index_in_dim(packed, lax.axis_index("fsdp"), 0, keepdims=False)
    return (
        section_out,
        section_in_grad,
        *big,
        packed[None, 0:2],
        packed[None, 2:4],
        packed[None, 4:6],
        packed[None, 6:8],
        packed[8:].reshape(1, -1),
    )


def solution(mesh):
    matrix = P("section", "fsdp", None)
    vectors = P("section", None, "fsdp")
    rows_out = P("section", "fsdp", "ctx", None)
    return jax.shard_map(
        shards,
        mesh=mesh,
        in_specs=(
            P("fsdp", "ctx", None),
            P("fsdp", None),
            P("fsdp", "ctx", None),
            *([matrix] * 4),
            *([vectors] * 4),
            P("section", "fsdp"),
        ),
        out_specs=(
            rows_out,
            rows_out,
            *([matrix] * 4),
            *([vectors] * 4),
            P("section", "fsdp"),
        ),
        check_vma=False,
    )
```

time: 2420 us -> 1090 us (0.45)
  waiting for transfers between devices: 1180 us -> 515 us
  matrix products: 668 us -> 205 us
  local copies, waits for them, and re-layouts: 264 us -> 71.8 us
  Pallas kernels: 0 us -> 98 us
  other arithmetic: 192 us -> 109 us
  blocking collectives: 71.8 us -> 36.5 us
    dot_general x84 -> x29, matrix products: 668 us -> 205 us  [the longest x8 68.1 us: mm_nt(): lax.dot_general(left, right, (((1,), (1,)), ((), ())), preferred_element_...]
    reduce_scatter x8 -> x0, waiting for transfers between devices: 439 us -> none  [the longest x4 290 us: attend_back(): lax.psum_scatter(joined.astype(jnp.bfloat16), 'ctx', scatter_dimension=1,...]
    all_gather x20 -> x6, waiting for transfers between devices: 532 us -> 134 us  [whole_weight(): gathered = lax.all_gather(piece, 'fsdp', axis=0)]
    psum x1 -> x2, waiting for transfers between devices: 122 us -> 257 us  [the longest x1 128 us: shards(): packed = lax.psum(packed, ('section', 'ctx', 'fsdp'))]
    pallas_call x0 -> x4, Pallas kernels: none -> 98 us  [the longest x2 51.1 us: attend_back(): pl.pallas_call(functools.partial(attend_back_kernel, query_block(length))...]
    all_gather x16 -> x0, local copies, waits for them, and re-layouts: 75.8 us -> none  [the longest x4 19.6 us: attend_forward(): key_piece = lax.all_gather(key_rows, 'ctx', axis=1, tiled=True)]
    all_to_all x0 -> x4, waiting for transfers between devices: none -> 70 us  [the longest x2 50.8 us: home(): moved = lax.all_to_all(both, 'ctx', 2, 2, tiled=True)]
    reduce_sum x19 -> x7, other arithmetic: 73.3 us -> 7.72 us  [row_sum(): return jnp.sum(rows.astype(f32), axis=0)]
  transfers between devices with their start and end apart: 39 -> 47, of which waited for: 30 -> 16; matrix products, arithmetic and copies ran while one was open for 35% -> 24% of each run, Pallas kernels for 0% -> 5%
where the time goes in v1:
time: 1090 us; the launch traced here: 1080 us
  waiting for transfers between devices  515 us (47%)
  matrix products  205 us (19%)
  other arithmetic  109 us (10%)
  Pallas kernels  98 us (9%)
  local copies, waits for them, and re-layouts  71.8 us (7%)
  blocking collectives  36.5 us (3%)
  starting transfers between devices  27.8 us (3%)
  between operations  16.5 us (2%)
    all_gather x6, waiting for transfers between devices, whole_weight(): gathered = lax.all_gather(piece, 'fsdp', axis=0)  134 us
    psum x1, waiting for transfers between devices, shards(): packed = lax.psum(packed, ('section', 'ctx', 'fsdp'))  128 us
    psum x1, waiting for transfers between devices, send(): return lax.psum(scattered, 'ctx')  128 us
    dot_general x8, matrix products, mm_nt(): lax.dot_general(left, right, (((1,), (1,)), ((), ())), preferred_element_...  68.1 us
    dot_general x8, matrix products, mm_tn(): lax.dot_general(left, right, (((0,), (0,)), ((), ())), preferred_element_...  58.5 us
    pallas_call x2, Pallas kernels, attend_back(): pl.pallas_call(functools.partial(attend_back_kernel, query_block(length))...  51.1 us
    all_to_all x2, waiting for transfers between devices, home(): moved = lax.all_to_all(both, 'ctx', 2, 2, tiled=True)  50.8 us
    pallas_call x2, Pallas kernels, attend_forward(): pl.pallas_call(functools.partial(attend_kernel, query_block(length)), gri...  47 us
  transfers between devices with their start and end apart: 47, of which 16 were waited for; matrix products, arithmetic and copies ran while one was open for 24% of the time, Pallas kernels for 5%

profile of v1, /device:TPU:0, one launch (start us, length us, event | category | flops | bytes accessed | tf_op | source)
XLA Modules:
  0.0 1079.5 jit_solution(12296838956624950229)
XLA Ops:
  20.7 2.9 fusion.84
  23.7 6.4 all-to-all-start
  30.2 8.2 all-gather.9
  42.4 12.3 %all-gather.2 = bf16[384,768]{1,0:T(8,128)(2,1)S(1)} all-gather(bf16[96,768]{1,0:T(8,128)(2,1)S(1)} %get-tuple-element.109), channel_id=4, replica_groups=mesh['section'=2,'ctx'=4,'fsdp'=4] {'fsdp'}, dimensions={0}, use_global_device_ids=true | all-gather | bytes 737280 | tf_op jit(solution)/shard_map/all_gather | solution.py:284
  54.7 12.3 %all-to-all-done = bf16[4,1,256,768]{3,2,1,0:T(8,128)(2,1)} async-done(((bf16[4,1,256,768]{3,2,1,0:T(8,128)(2,1)}), bf16[4,1,256,768]{3,2,1,0:T(8,128)(2,1)}, u32[]{:S(2)}, u32[]{:S(2)}) %all-to-all-start) | async-done | bytes 1572896 | tf_op jit(solution)/shard_map/all_to_all | solution.py:296
  67.1 4.4 all-to-all-start.2
  71.5 15.9 %all-gather.6 = bf16[384,768]{1,0:T(8,128)(2,1)S(1)} all-gather(bf16[96,768]{1,0:T(8,128)(2,1)S(1)} %get-tuple-element.108), channel_id=8, replica_groups=mesh['section'=2,'ctx'=4,'fsdp'=4] {'fsdp'}, dimensions={0}, use_global_device_ids=true | all-gather | bytes 737280 | tf_op jit(solution)/shard_map/all_gather | solution.py:284
  97.2 3.3 convert_reduce_fusion.3
  101.1 6.9 all-to-all-done.2
  108.0 4.6 fusion.69
  112.6 15.0 %all-gather.19.cloned.1.call-done = bf16[384,3072]{1,0:T(8,128)(2,1)} async-done(((bf16[96,3072]{1,0:T(8,128)(2,1)}), bf16[384,3072]{1,0:T(8,128)(2,1)}) %all-gather.19.cloned.1.call-update) | async-done | bytes 2359312 | tf_op jit(solution)/shard_map/all_gather | solution.py:284
  127.5 39.8 %all-gather.25.cloned.1.call-done = bf16[384,3072]{1,0:T(8,128)(2,1)} async-done(((bf16[96,3072]{1,0:T(8,128)(2,1)}), bf16[384,3072]{1,0:T(8,128)(2,1)}) %all-gather.25.cloned.1.call-update) | async-done | bytes 2359312 | tf_op jit(solution)/shard_map/all_gather | solution.py:284
  167.3 39.8 %all-gather.21.cloned.1.call-done = bf16[1536,768]{1,0:T(8,128)(2,1)} async-done(((bf16[384,768]{1,0:T(8,128)(2,1)}), bf16[1536,768]{1,0:T(8,128)(2,1)}) %all-gather.21.cloned.1.call-update) | async-done | bytes 2359312 | tf_op jit(solution)/shard_map/all_gather | solution.py:284
  207.1 39.8 %all-gather.27.cloned.1.call-done = bf16[1536,768]{1,0:T(8,128)(2,1)} async-done(((bf16[384,768]{1,0:T(8,128)(2,1)}), bf16[1536,768]{1,0:T(8,128)(2,1)}) %all-gather.27.cloned.1.call-update) | async-done | bytes 2359312 | tf_op jit(solution)/shard_map/all_gather | solution.py:284
  250.7 4.7 add_convert_fusion.1.q_ref.k_ref.v_ref
  255.5 23.5 %shard_map.203 = (bf16[1024,768]{1,0:T(8,128)(2,1)S(1)}, f32[1,6,2,1024]{3,2,1,0:T(2,128)S(1)}) custom-call(bf16[1024,2304]{1,0:T(8,128)(2,1)S(1)} %add_convert_fusion.1.q_ref.k_ref.v_ref, bf16[1024,2304]{1,0:T(8,128)(2,1)S(1)} %add_convert_fusion.1.q_ref.k_ref.v_ref, bf16[1024,2304]{1,0:T(8,128)(2,1)S(1)} %add_convert_fusion.1.q_ref.k_ref.v_ref), custom_call_target="tpu_custom_call" | custom-call | flops 6442450944 | bytes 6291456 | tf_op jit(solution)/shard_map/pallas_call | solution.py:116
  281.1 2.5 select_bitcast_fusion.15
  300.8 2.7 pad_maximum_fusion.1
  303.5 8.7 fusion.102
  312.3 11.7 %convert_reduce_fusion.2 = (f32[1024]{0:T(1024)S(1)}, bf16[1024,768]{0,1:T(8,128)(2,1)S(1)}) fusion(f32[768]{0:T(1024)S(1)} %copy-done.132, f32[1024,768]{0,1:T(8,128)S(1)} %get-tuple-element.121, bf16[3072,768]{1,0:T(8,128)(2,1)} %bitcast.389, f32[1024,3072]{1,0:T(8,128)} %fusion.102, f32[3072]{0:T(1024)S(1)} %copy-done.118), kind=kOutput, calls=%fused_computation.36 | convolution fusion | flops 4867226624 | bytes 22039552 | tf_op jit(solution)/shard_map/dot_general | solution.py:32
  324.5 4.5 add_convert_fusion.q_ref.k_ref.v_ref
  329.0 23.5 %shard_map.204 = (bf16[1024,768]{1,0:T(8,128)(2,1)S(1)}, f32[1,6,2,1024]{3,2,1,0:T(2,128)S(1)}) custom-call(bf16[1024,2304]{1,0:T(8,128)(2,1)S(1)} %add_convert_fusion.q_ref.k_ref.v_ref, bf16[1024,2304]{1,0:T(8,128)(2,1)S(1)} %add_convert_fusion.q_ref.k_ref.v_ref, bf16[1024,2304]{1,0:T(8,128)(2,1)S(1)} %add_convert_fusion.q_ref.k_ref.v_ref), custom_call_target="tpu_custom_call" | custom-call | flops 6442450944 | bytes 6291456 | tf_op jit(solution)/shard_map/pallas_call | solution.py:116
  354.7 8.8 fusion.103
  363.6 17.0 %convert_reduce_fusion = (f32[3072]{0:T(1024)}, bf16[1024,3072]{1,0:T(8,128)(2,1)}) fusion(f32[1024,3072]{1,0:T(8,128)} %fusion.103, f32[3072]{0:T(1024)S(1)} %copy-done.116, bf16[1024,768]{0,1:T(8,128)(2,1)S(1)} %copy-done.41, bf16[3072,768]{1,0:T(8,128)(2,1)S(1)} %bitcast.388), kind=kOutput, calls=%fused_computation.18 | convolution fusion | flops 4904186880 | bytes 25190400 | tf_op jit(solution)/shard_map/dot_general | solution.py:36
  380.6 9.0 fusion.111
  389.6 3.7 copy.136
  393.4 4.5 multiply_reduce_fusion
  404.2 25.5 %shard_map.205 = (bf16[1024,768]{1,0:T(8,128)(2,1)S(1)}, bf16[1024,768]{1,0:T(8,128)(2,1)S(1)}, bf16[1024,768]{1,0:T(8,128)(2,1)S(1)}) custom-call(bf16[1024,2304]{1,0:T(8,128)(2,1)S(1)} %bitcast.354, bf16[1024,2304]{1,0:T(8,128)(2,1)S(1)} %bitcast.354, bf16[1024,2304]{1,0:T(8,128)(2,1)S(1)} %bitcast.354, ...), custom_call_target="tpu_custom_call" | custom-call | flops 16106127360 | bytes 12582912 | tf_op jit(solution)/shard_map/pallas_call | solution.py:138
  432.9 6.2 fusion.110
  439.0 4.9 convolution_convert_fusion.4
  453.8 3.0 convert_reduce_fusion.4
  456.8 16.7 %convert_reduce_fusion.1 = (f32[3072]{0:T(1024)}, bf16[1024,3072]{1,0:T(8,128)(2,1)S(1)}) fusion(f32[1024,3072]{1,0:T(8,128)} %fusion.102, f32[3072]{0:T(1024)S(1)} %copy-done.118, bf16[1024,768]{0,1:T(8,128)(2,1)S(1)} %get-tuple-element.64, bf16[3072,768]{1,0:T(8,128)(2,1)} %bitcast.390), kind=kOutput, calls=%fused_computation.19 | convolution fusion | flops 4904186880 | bytes 25190400 | tf_op jit(solution)/shard_map/dot_general | solution.py:36
  473.5 7.3 fusion.113
  480.8 3.9 copy.138
  484.8 3.5 multiply_reduce_fusion.1
  495.4 2.6 convolution_convert_fusion.6.do_ref
  505.4 25.5 %shard_map.206 = (bf16[1024,768]{1,0:T(8,128)(2,1)S(1)}, bf16[1024,768]{1,0:T(8,128)(2,1)S(1)}, bf16[1024,768]{1,0:T(8,128)(2,1)S(1)}) custom-call(bf16[1024,2304]{1,0:T(8,128)(2,1)S(1)} %copy-done.14, bf16[1024,2304]{1,0:T(8,128)(2,1)S(1)} %copy-done.14, bf16[1024,2304]{1,0:T(8,128)(2,1)S(1)} %copy-done.14, bf16[1024,768]{1,0:T(8,128)(2,1)S(1)} %copy-done.12, ...), custom_call_target="tpu_custom_call" | custom-call | flops 16106127360 | bytes 12582912 | tf_op jit(solution)/shard_map/pallas_call | solution.py:138
  532.1 2.5 fusion.89
  539.8 3.3 fusion.44
  543.3 7.1 convolution_convert_fusion.5
  550.9 3.4 collective-permute-done.15
  556.2 11.6 %convolution_convert_fusion = bf16[3072,768]{1,0:T(8,128)(2,1)S(1)} fusion(bf16[1024,768]{0,1:T(8,128)(2,1)S(1)} %copy-done.44, f32[1024,3072]{1,0:T(8,128)} %fusion.103, f32[3072]{0:T(1024)S(1)} %copy-done.117), kind=kOutput, calls=%fused_computation.24 | convolution fusion | flops 4865654784 | bytes 18886656 | tf_op jit(solution)/shard_map/dot_general | solution.py:40
  571.1 4.5 collective-permute-done.25
  575.6 5.6 fusion.22
  581.4 8.8 convolution_convert_fusion.2
  591.6 13.1 %convolution_convert_fusion.1 = bf16[3072,768]{1,0:T(8,128)(2,1)} fusion(bf16[1024,768]{0,1:T(8,128)(2,1)S(1)} %copy-done.47, f32[1024,3072]{1,0:T(8,128)} %fusion.102, f32[3072]{0:T(1024)S(1)} %copy-done.118), kind=kOutput, calls=%fused_computation.25 | convolution fusion | flops 4865654784 | bytes 18886656 | tf_op jit(solution)/shard_map/dot_general | solution.py:40
  604.7 2.7 fusion.24
  607.6 4.0 select_bitcast_fusion.1
  612.0 16.9 %fusion.75 = bf16[1024,768]{1,0:T(8,128)(2,1)} fusion(s32[1024]{0:T(1024)S(1)} %bitcast.428, f32[1024,768]{0,1:T(8,128)S(1)} %copy-done.21, bf16[3072,768]{1,0:T(8,128)(2,1)} %bitcast.385, f32[768]{0:T(1024)S(1)} %add.330, f32[1024,3072]{1,0:T(8,128)} %fusion.103, f32[3072]{0:T(1024)S(1)} %copy-done.117), kind=kOutput, calls=%fused_computation.161 | convolution fusion | flops 6479151104 | bytes 22039552 | tf_op jit(solution)/shard_map/bpt,bpd->btd/dot_general | solution.py:313
  628.9 3.4 fusion.72
  635.3 10.2 convolution_convert_fusion.3
  645.5 4.2 fusion.23
  649.8 4.3 select_bitcast_fusion.3
  654.2 7.8 fusion.112
  662.1 2.7 copy.139
  672.4 4.7 all-to-all-start.1
  677.4 6.6 fusion.78
  684.0 5.9 fusion.25
  692.3 3.1 collective-permute-done.14
  697.7 50.8 %all-to-all-done.1 = bf16[2,1,4,256,768]{4,3,1,0,2:T(8,128)(2,1)} async-done(((bf16[2,1,4,256,768]{4,3,1,0,2:T(8,128)(2,1)}), bf16[2,1,4,256,768]{4,3,1,0,2:T(8,128)(2,1)}, u32[]{:S(2)}, u32[]{:S(2)}) %all-to-all-start.1) | async-done | bytes 3145760 | tf_op jit(solution)/shard_map/all_to_all | solution.py:322
  748.5 4.7 all-to-all-start.3
  758.4 36.9 %reduce-scatter.33.cloned.1.call-done = bf16[1,96,3072]{2,1,0:T(8,128)(2,1)} async-done(((bf16[4,96,3072]{2,1,0:T(8,128)(2,1)}), bf16[1,96,3072]{2,1,0:T(8,128)(2,1)}) %reduce-scatter.33.cloned.1.call-update) | async-done | bytes 589840
  795.3 128.5 %all-reduce.15.cloned.1.call-done = f32[2,4,12,192]{3,2,1,0:T(8,128)} async-done(((f32[2,4,12,192]{3,2,1,0:T(8,128)}), f32[2,4,12,192]{3,2,1,0:T(8,128)}) %all-reduce.15.cloned.1.call-update) | async-done | bytes 73744 | tf_op jit(solution)/shard_map/psum | solution.py:364
  933.9 128.0 %all-reduce.17.cloned.1.call-done = (bf16[96,2304]{1,0:T(8,128)(2,1)}, bf16[96,2304]{1,0:T(8,128)(2,1)}, bf16[96,768]{1,0:T(8,128)(2,1)}, bf16[96,768]{1,0:T(8,1...) async-done(((bf16[96,2304]{1,0:T(8,128)(2,1)}, bf16[96,2304]{1,0:T(8,128)(2,1)}, ...) | async-done | bytes 3538960 | tf_op jit(solution)/shard_map/psum | solution.py:339
  (551 shorter events, 142.1 us)
Async XLA Ops:
  7.2 87.2 %all-gather.17.cloned.1.call-start = ((), (), s32[]{:S(2)}) async-start(), calls=%async_computation.13 | async-start | bytes 2211840 | tf_op jit(solution)/shard_map/all_gather | solution.py:284
  8.5 1.9 collective-permute-start.1
  12.6 99.9 %all-gather.23.cloned.1.call-start = ((), (), s32[]{:S(2)}) async-start(), calls=%async_computation.16 | async-start | bytes 2211840 | tf_op jit(solution)/shard_map/all_gather | solution.py:284
  13.4 114.2 %all-gather.19.cloned.1.call-start = ((), (), s32[]{:S(2)}) async-start(), calls=%async_computation.14 | async-start | bytes 2949120 | tf_op jit(solution)/shard_map/all_gather | solution.py:284
  13.5 2.1 collective-permute-start.5
  16.7 150.6 %all-gather.25.cloned.1.call-start = ((), (), s32[]{:S(2)}) async-start(), calls=%async_computation.17 | async-start | bytes 2949120 | tf_op jit(solution)/shard_map/all_gather | solution.py:284
  17.3 189.8 %all-gather.21.cloned.1.call-start = ((), (), s32[]{:S(2)}) async-start(), calls=%async_computation.15 | async-start | bytes 2949120 | tf_op jit(solution)/shard_map/all_gather | solution.py:284
  17.4 2.1 collective-permute-start.7
  23.7 43.4 %all-to-all-start = ((bf16[4,1,256,768]{3,2,1,0:T(8,128)(2,1)}), bf16[4,1,256,768]{3,2,1,0:T(8,128)(2,1)}, u32[]{:S(2)}, u32[]{:S(2)}) async-start(bf16[4,1,256,768]{3,2,1,0:T(8,128)(2,1)} %fusion.84), calls=%async_computation | async-start | bytes 3145728 | tf_op jit(solution)/shard_map/all_to_all | solution.py:296
  30.0 216.8 %all-gather.27.cloned.1.call-start = ((), (), s32[]{:S(2)}) async-start(), calls=%async_computation.18 | async-start | bytes 2949120 | tf_op jit(solution)/shard_map/all_gather | solution.py:284
  38.4 2.5 collective-permute-start
  38.5 3.9 collective-permute-start.3
  54.7 39.4 %collective-permute-start.4 = (bf16[4,96,768]{2,1,0:T(8,128)(2,1)S(1)}, bf16[4,96,768]{2,1,0:T(8,128)(2,1)S(1)}, u32[]{:S(2)}, u32[]{:S(2)}) collective-permute-start(bf16[4,96,768]{2,1,0:T(8,128)(2,1)S(1)} %bitcast.395), channel_id=1, source_target_pairs={{0,16},{16,0},{1,17},{17,1},{2,18},{18,2},{3,19},{19,3},{4,20},{20... | collective-permute-start | bytes 1769480 | tf_op jit(solution)/shard_map/ppermute | solution.py:227
  67.1 40.9 %all-to-all-start.2 = ((bf16[4,1,256,768]{3,2,1,0:T(8,128)(2,1)}), bf16[4,1,256,768]{3,2,1,0:T(8,128)(2,1)}, u32[]{:S(2)}, u32[]{:S(2)}) async-start(bf16[4,1,256,768]{3,2,1,0:T(8,128)(2,1)} %fusion.85), calls=%async_computation.2 | async-start | bytes 3145728 | tf_op jit(solution)/shard_map/all_to_all | solution.py:296
  71.5 686.8 %reduce-scatter.31.cloned.1.call-start = ((), (), s32[]{:S(2)}) async-start(), calls=%async_computation.22 | async-start | bytes 737280
  87.5 6.8 collective-permute-start.10
  88.2 309.7 %copy-start.86 = (f32[768]{0:T(1024)}, f32[768]{0:T(1024)S(1)}, u32[]{:S(2)}) copy-start(f32[768]{0:T(1024)S(1)} %mul.361) | copy-start | bytes 9220
  88.9 265.7 %copy-start.94 = (f32[768]{0:T(1024)}, f32[768]{0:T(1024)S(1)}, u32[]{:S(2)}) copy-start(f32[768]{0:T(1024)S(1)} %add.322) | copy-start | bytes 9220
  90.6 212.9 %copy-start.84 = (f32[768]{0:T(1024)}, f32[768]{0:T(1024)S(1)}, u32[]{:S(2)}) copy-start(f32[768]{0:T(1024)S(1)} %mul.345) | copy-start | bytes 9220
  91.4 212.1 %copy-start.92 = (f32[768]{0:T(1024)}, f32[768]{0:T(1024)S(1)}, u32[]{:S(2)}) copy-start(f32[768]{0:T(1024)S(1)} %add.300) | copy-start | bytes 9220
  94.3 152.5 %collective-permute-start.2 = (bf16[4,96,2304]{2,1,0:T(8,128)(2,1)}, bf16[4,96,2304]{2,1,0:T(8,128)(2,1)}, u32[]{:S(2)}, u32[]{:S(2)}) collective-permute-start(bf16[4,96,2304]{2,1,0:T(8,128)(2,1)} %bitcast.409), channel_id=1, source_target_pairs={{0,16},{16,0},{1,17},{17,1},{2,18},{18,2},{3,19},{19,3},{4,20},{20... | collective-permute-start | bytes 5308424 | tf_op jit(solution)/shard_map/ppermute | solution.py:227
  100.6 178.4 %copy-start.32 = (bf16[1024,768]{0,1:T(8,128)(2,1)}, bf16[1024,768]{0,1:T(8,128)(2,1)S(1)}, u32[]{:S(2)}) copy-start(bf16[1024,768]{0,1:T(8,128)(2,1)S(1)} %get-tuple-element.119) | copy-start | bytes 4718596
  100.6 148.3 %copy-start.96 = (f32[1024]{0:T(1024)}, f32[1024]{0:T(1024)S(1)}, u32[]{:S(2)}) copy-start(f32[1024]{0:T(1024)S(1)} %broadcast_multiply_fusion.3) | copy-start | bytes 12292
  101.1 147.9 %copy-start.106 = (f32[1024]{0:T(1024)}, f32[1024]{0:T(1024)S(1)}, u32[]{:S(2)}) copy-start(f32[1024]{0:T(1024)S(1)} %fusion.94) | copy-start | bytes 12292
  108.0 138.9 %copy-start.69 = (bf16[384,2304]{1,0:T(8,128)(2,1)S(1)}, bf16[384,2304]{1,0:T(8,128)(2,1)}, u32[]{:S(2)}) copy-start(bf16[384,2304]{1,0:T(8,128)(2,1)} %all-gather.17.cloned.1.call-done) | copy-start | bytes 5308420
  112.6 168.2 %collective-permute-start.9 = (bf16[4,96,2304]{2,1,0:T(8,128)(2,1)}, bf16[4,96,2304]{2,1,0:T(8,128)(2,1)}, u32[]{:S(2)}, u32[]{:S(2)}) collective-permute-start(bf16[4,96,2304]{2,1,0:T(8,128)(2,1)} %bitcast.407), channel_id=1, source_target_pairs={{0,16},{16,0},{1,17},{17,1},{2,18},{18,2},{3,19},{19,3},{4,20},{20... | collective-permute-start | bytes 5308424 | tf_op jit(solution)/shard_map/ppermute | solution.py:227
  127.5 166.9 %collective-permute-start.6 = (bf16[4,96,3072]{2,1,0:T(8,128)(2,1)}, bf16[4,96,3072]{2,1,0:T(8,128)(2,1)}, u32[]{:S(2)}, u32[]{:S(2)}) collective-permute-start(bf16[4,96,3072]{2,1,0:T(8,128)(2,1)} %bitcast.399), channel_id=1, source_target_pairs={{0,16},{16,0},{1,17},{17,1},{2,18},{18,2},{3,19},{19,3},{4,20},{20... | collective-permute-start | bytes 7077896 | tf_op jit(solution)/shard_map/ppermute | solution.py:227
  167.3 119.1 %collective-permute-start.11 = (bf16[4,96,3072]{2,1,0:T(8,128)(2,1)}, bf16[4,96,3072]{2,1,0:T(8,128)(2,1)}, u32[]{:S(2)}, u32[]{:S(2)}) collective-permute-start(bf16[4,96,3072]{2,1,0:T(8,128)(2,1)} %bitcast.403), channel_id=1, source_target_pairs={{0,16},{16,0},{1,17},{17,1},{2,18},{18,2},{3,19},{19,3},{4,20},{20... | collective-permute-start | bytes 7077896 | tf_op jit(solution)/shard_map/ppermute | solution.py:227
  207.1 89.9 %collective-permute-start.8 = (bf16[4,384,768]{2,1,0:T(8,128)(2,1)}, bf16[4,384,768]{2,1,0:T(8,128)(2,1)}, u32[]{:S(2)}, u32[]{:S(2)}) collective-permute-start(bf16[4,384,768]{2,1,0:T(8,128)(2,1)} %bitcast.401), channel_id=1, source_target_pairs={{0,16},{16,0},{1,17},{17,1},{2,18},{18,2},{3,19},{19,3},{4,20},{20... | collective-permute-start | bytes 7077896 | tf_op jit(solution)/shard_map/ppermute | solution.py:227
  246.9 43.0 %collective-permute-start.12 = (bf16[4,384,768]{2,1,0:T(8,128)(2,1)}, bf16[4,384,768]{2,1,0:T(8,128)(2,1)S(1)}, u32[]{:S(2)}, u32[]{:S(2)}) collective-permute-start(bf16[4,384,768]{2,1,0:T(8,128)(2,1)} %bitcast.405), channel_id=1, source_target_pairs={{0,16},{16,0},{1,17},{17,1},{2,18},{18,2},{3,19},{19,3},{4,20},{20... | collective-permute-start | bytes 7077896 | tf_op jit(solution)/shard_map/ppermute | solution.py:227
  324.0 115.0 %copy-start.26 = (bf16[1024,768]{0,1:T(8,128)(2,1)}, bf16[1024,768]{0,1:T(8,128)(2,1)S(1)}, u32[]{:S(2)}) copy-start(bf16[1024,768]{0,1:T(8,128)(2,1)S(1)} %get-tuple-element.123) | copy-start | bytes 4718596
  354.2 43.6 %copy-start.81 = (f32[1024]{0:T(1024)}, f32[1024]{0:T(1024)S(1)}, u32[]{:S(2)}) copy-start(f32[1024]{0:T(1024)S(1)} %broadcast_multiply_fusion) | copy-start | bytes 12292
  354.7 43.2 %copy-start.90 = (f32[1024]{0:T(1024)}, f32[1024]{0:T(1024)S(1)}, u32[]{:S(2)}) copy-start(f32[1024]{0:T(1024)S(1)} %fusion.97) | copy-start | bytes 12292
  444.9 53.1 %collective-permute-start.19 = (bf16[4,96,768]{2,1,0:T(8,128)(2,1)}, bf16[4,96,768]{2,1,0:T(8,128)(2,1)}, u32[]{:S(2)}, u32[]{:S(2)}) collective-permute-start(bf16[4,96,768]{2,1,0:T(8,128)(2,1)} %select_bitcast_fusion.24), channel_id=1, source_target_pairs={{0,16},{16,0},{1,17},{17,1},{2,18},{18,2},{3,19},{19,3},{4,20},{20... | collective-permute-start | bytes 1769480 | tf_op jit(solution)/shard_map/ppermute | solution.py:227
  446.8 92.0 %collective-permute-start.16 = (bf16[4,96,2304]{2,1,0:T(8,128)(2,1)}, bf16[4,96,2304]{2,1,0:T(8,128)(2,1)}, u32[]{:S(2)}, u32[]{:S(2)}) collective-permute-start(bf16[4,96,2304]{2,1,0:T(8,128)(2,1)} %select_bitcast_fusion.12), channel_id=1, source_target_pairs={{0,16},{16,0},{1,17},{17,1},{2,18},{18,2},{3,19},{19,3},{4,20},{20... | collective-permute-start | bytes 5308424 | tf_op jit(solution)/shard_map/ppermute | solution.py:227
  495.1 36.9 %collective-permute-start.18 = (bf16[4,96,768]{2,1,0:T(8,128)(2,1)}, bf16[4,96,768]{2,1,0:T(8,128)(2,1)}, u32[]{:S(2)}, u32[]{:S(2)}) collective-permute-start(bf16[4,96,768]{2,1,0:T(8,128)(2,1)} %select_bitcast_fusion.25), channel_id=1, source_target_pairs={{0,16},{16,0},{1,17},{17,1},{2,18},{18,2},{3,19},{19,3},{4,20},{20... | collective-permute-start | bytes 1769480 | tf_op jit(solution)/shard_map/ppermute | solution.py:227
  500.2 258.1 %reduce-scatter.29.cloned.1.call-start = ((), (), s32[]{:S(2)}) async-start(), calls=%async_computation.21 | async-start | bytes 737280
  534.7 223.7 %reduce-scatter.27.cloned.1.call-start = ((), (), s32[]{:S(2)}) async-start(), calls=%async_computation.20 | async-start | bytes 2211840
  543.2 215.2 %reduce-scatter.25.cloned.1.call-start = ((), (), s32[]{:S(2)}) async-start(), calls=%async_computation.19 | async-start | bytes 2211840
  550.5 3.8 collective-permute-start.15
  556.2 202.2 %reduce-scatter.39.cloned.1.call-start = ((), (), s32[]{:S(2)}) async-start(), calls=%async_computation.26 | async-start | bytes 2949120
  570.7 4.9 collective-permute-start.25
  581.3 177.1 %reduce-scatter.35.cloned.1.call-start = ((), (), s32[]{:S(2)}) async-start(), calls=%async_computation.24 | async-start | bytes 2949120
  590.4 14.2 %collective-permute-start.22 = (bf16[4,96,3072]{2,1,0:T(8,128)(2,1)S(1)}, bf16[4,96,3072]{2,1,0:T(8,128)(2,1)S(1)}, u32[]{:S(2)}, u32[]{:S(2)}) collective-permute-start(bf16[4,96,3072]{2,1,0:T(8,128)(2,1)S(1)} %select_bitcast_fusion.2), channel_id=1, source_target_pairs={{0,16},{16,0},{1,17},{17,1},{2,18},{18,2},{3,19},{19,3},{4,20},{20... | collective-permute-start | bytes 7077896 | tf_op jit(solution)/shard_map/ppermute | solution.py:227
  607.4 151.0 %reduce-scatter.37.cloned.1.call-start = ((), (), s32[]{:S(2)}) async-start(), calls=%async_computation.25 | async-start | bytes 2949120
  611.7 33.9 %collective-permute-start.24 = (bf16[4,384,768]{2,1,0:T(8,128)(2,1)}, bf16[4,384,768]{2,1,0:T(8,128)(2,1)}, u32[]{:S(2)}, u32[]{:S(2)}) collective-permute-start(bf16[4,384,768]{2,1,0:T(8,128)(2,1)} %select_bitcast_fusion.1), channel_id=1, source_target_pairs={{0,16},{16,0},{1,17},{17,1},{2,18},{18,2},{3,19},{19,3},{4,20},{20... | collective-permute-start | bytes 7077896 | tf_op jit(solution)/shard_map/ppermute | solution.py:227
  634.0 34.3 %collective-permute-start.13 = (bf16[1,1024,768]{2,1,0:T(8,128)(2,1)}, bf16[1,1024,768]{2,1,0:T(8,128)(2,1)}, u32[]{:S(2)}, u32[]{:S(2)}) collective-permute-start(bf16[1,1024,768]{2,1,0:T(8,128)(2,1)} %select_bitcast_fusion.19), channel_id=1, source_target_pairs={{0,16},{16,0},{1,17},{17,1},{2,18},{18,2},{3,19},{19,3},{4,20},{20... | collective-permute-start | bytes 4718600 | tf_op jit(solution)/shard_map/ppermute | solution.py:227
  654.1 29.9 %collective-permute-start.21 = (bf16[4,96,3072]{2,1,0:T(8,128)(2,1)}, bf16[4,96,3072]{2,1,0:T(8,128)(2,1)}, u32[]{:S(2)}, u32[]{:S(2)}) collective-permute-start(bf16[4,96,3072]{2,1,0:T(8,128)(2,1)} %select_bitcast_fusion.3), channel_id=1, source_target_pairs={{0,16},{16,0},{1,17},{17,1},{2,18},{18,2},{3,19},{19,3},{4,20},{20... | collective-permute-start | bytes 7077896 | tf_op jit(solution)/shard_map/ppermute | solution.py:227
  672.4 76.1 %all-to-all-start.1 = ((bf16[2,1,4,256,768]{4,3,1,0,2:T(8,128)(2,1)}), bf16[2,1,4,256,768]{4,3,1,0,2:T(8,128)(2,1)}, u32[]{:S(2)}, u32[]{:S(2)}) async-start(bf16[2,1,4,256,768]{4,3,1,0,2:T(8,128)(2,1)} %pad_maximum_fusion.6), calls=%async_computation.1 | async-start | bytes 6291456 | tf_op jit(solution)/shard_map/all_to_all | solution.py:322
  677.1 118.2 %reduce-scatter.33.cloned.1.call-start = ((), (), s32[]{:S(2)}) async-start(), calls=%async_computation.23 | async-start | bytes 2949120
  692.0 3.5 collective-permute-start.14
  697.7 55.7 %copy-start.127 = (f32[768]{0:T(1024)S(1)}, f32[768]{0:T(1024)}, u32[]{:S(2)}) copy-start(f32[768]{0:T(1024)} %get-tuple-element.130) | copy-start | bytes 9220
  697.7 55.8 %copy-start.119 = (f32[3072]{0:T(1024)S(1)}, f32[3072]{0:T(1024)}, u32[]{:S(2)}) copy-start(f32[3072]{0:T(1024)} %get-tuple-element.126) | copy-start | bytes 36868
  697.7 55.8 %copy-start.114 = (f32[768]{0:T(1024)S(1)}, f32[768]{0:T(1024)}, u32[]{:S(2)}) copy-start(f32[768]{0:T(1024)} %get-tuple-element.33) | copy-start | bytes 9220
  697.7 55.9 %copy-start.108 = (f32[768]{0:T(1024)S(1)}, f32[768]{0:T(1024)}, u32[]{:S(2)}) copy-start(f32[768]{0:T(1024)} %get-tuple-element.67) | copy-start | bytes 9220
  697.7 56.0 %copy-start.3 = (bf16[1024,768]{1,0:T(8,128)(2,1)S(1)}, bf16[1024,768]{1,0:T(8,128)(2,1)}, u32[]{:S(2)}) copy-start(bf16[1024,768]{1,0:T(8,128)(2,1)} %copy-done.2) | copy-start | bytes 4718596
  697.7 56.4 %copy-start.1 = (bf16[1024,768]{1,0:T(8,128)(2,1)S(1)}, bf16[1024,768]{1,0:T(8,128)(2,1)}, u32[]{:S(2)}) copy-start(bf16[1024,768]{1,0:T(8,128)(2,1)} %copy-done) | copy-start | bytes 4718596
  748.5 180.2 %all-to-all-start.3 = ((bf16[2,1,4,256,768]{4,3,1,0,2:T(8,128)(2,1)}), bf16[2,1,4,256,768]{4,3,1,0,2:T(8,128)(2,1)}, u32[]{:S(2)}, u32[]{:S(2)}) async-start(bf16[2,1,4,256,768]{4,3,1,0,2:T(8,128)(2,1)} %pad_maximum_fusion.7), calls=%async_computation.3 | async-start | bytes 6291456 | tf_op jit(solution)/shard_map/all_to_all | solution.py:322
  753.3 170.5 %all-reduce.15.cloned.1.call-start = ((), (), s32[]{:S(2)}) async-start(), calls=%async_computation.12 | async-start | bytes 262144 | tf_op jit(solution)/shard_map/psum | solution.py:364
  758.2 303.8 %all-reduce.17.cloned.1.call-start = ((), (), s32[]{:S(2)}) async-start(), calls=%async_computation.27 | async-start | bytes 7077888 | tf_op jit(solution)/shard_map/psum | solution.py:339
  1063.0 3.6 collective-permute-start.20
  1064.3 3.3 collective-permute-start.17
  1066.0 4.8 collective-permute-start.26
  1066.1 2.9 collective-permute-start.23
  (131 other events, 897.1 us)
Sparse Core Ops, SparseCore 0:
  12.7 36.5 all-gather.16
  51.2 36.9 all-gather.22
  90.0 37.4 all-gather.18
  129.8 37.4 all-gather.24
  169.6 37.4 all-gather.20
  209.3 37.4 all-gather.26
  500.3 25.0 reduce-scatter.30
  534.8 25.0 reduce-scatter.28
  563.5 32.4 reduce-scatter.26
  598.9 32.4 reduce-scatter.24
  635.0 37.3 reduce-scatter.38
  675.9 37.3 reduce-scatter.34
  717.0 37.3 reduce-scatter.36
  757.9 37.3 reduce-scatter.32
  800.7 123.0 all-reduce.14
  926.6 135.3 all-reduce.16

commit v2 on v1

--- a/solution.py
+++ b/solution.py
@@ -183,24 +183,36 @@
     w_qkv, w_proj, w_fc, w_out = weights
     gains, offsets, attn_bias, out_bias, fc_bias = smalls
     layer_in, normed, project, mixed, log_total, after, normed_two, inner, active = kept
-    grad_w_out = send(mm_tn(active, grad_out).astype(bf16))
+    grad_out, grad_w_out = lax.optimization_barrier(
+        (grad_out, mm_tn(active, grad_out).astype(bf16))
+    )
+    grad_w_out = send(grad_w_out)
     grad_bias_two = row_sum(grad_out)
     grad_active = mm_nt(grad_out, w_out)
     _, gelu_pull = jax.vjp(gelu_tanh, inner)
     grad_inner = gelu_pull(grad_active)[0].astype(bf16)
-    grad_w_fc = send(mm_tn(normed_two, grad_inner).astype(bf16))
+    grad_inner, grad_w_fc = lax.optimization_barrier(
+        (grad_inner, mm_tn(normed_two, grad_inner).astype(bf16))
+    )
+    grad_w_fc = send(grad_w_fc)
     grad_fc_bias = row_sum(grad_inner)
     grad_normed_two = mm_nt(grad_inner, w_fc)
     _, norm_pull = jax.vjp(layer_norm, after, gains[1], offsets[1])
     grad_after, grad_gain_two, grad_offset_two = norm_pull(grad_normed_two)
     grad_after = grad_after + grad_out.astype(f32)
     grad_branch = grad_after.astype(bf16)
-    grad_w_proj = send(mm_tn(mixed, grad_branch).astype(bf16))
+    grad_branch, grad_w_proj = lax.optimization_barrier(
+        (grad_branch, mm_tn(mixed, grad_branch).astype(bf16))
+    )
+    grad_w_proj = send(grad_w_proj)
     grad_bias_one = row_sum(grad_branch)
     grad_mixed = mm_nt(grad_branch, w_proj).astype(bf16)
     grad_q, grad_k, grad_v = attend_back(project, grad_mixed, mixed, log_total, length)
     grad_project = jnp.concatenate([grad_q, grad_k, grad_v], axis=-1)
-    grad_w_qkv = send(mm_tn(normed, grad_project).astype(bf16))
+    grad_project, grad_w_qkv = lax.optimization_barrier(
+        (grad_project, mm_tn(normed, grad_project).astype(bf16))
+    )
+    grad_w_qkv = send(grad_w_qkv)
     grad_normed = mm_nt(grad_project, w_qkv)
     _, first_pull = jax.vjp(layer_norm, layer_in.astype(f32), gains[0], offsets[0])
     grad_hidden, grad_gain_one, grad_offset_one = first_pull(grad_normed)
@@ -225,6 +237,58 @@
 
 def swap(value):
     return lax.ppermute(value, "section", [(0, 1), (1, 0)])
+
+
+def cross(value, bit):
+    return lax.ppermute(value, "fsdp", [(i, i ^ bit) for i in range(4)])
+
+
+def add(left, right):
+    return (left.astype(f32) + right.astype(f32)).astype(left.dtype)
+
+
+def gather_fsdp(shard):
+    if lax.axis_size("fsdp") != 4:
+        return lax.all_gather(shard, "fsdp", axis=0)
+    half = shard.shape[0] // 2
+    near = cross(shard, 1)
+    far = cross(shard, 2)
+    corner = jnp.concatenate([cross(far[:half], 1), cross(near[half:], 2)], axis=0)
+    index = lax.axis_index("fsdp")
+    even, low = index % 2 == 0, index < 2
+    a, b = jnp.where(even, shard, near), jnp.where(even, near, shard)
+    c, d = jnp.where(even, far, corner), jnp.where(even, corner, far)
+    return jnp.stack(
+        [jnp.where(low, a, c), jnp.where(low, b, d), jnp.where(low, c, a), jnp.where(low, d, b)]
+    )
+
+
+def scatter_fsdp(parts):
+    if lax.axis_size("fsdp") != 4:
+        return lax.psum_scatter(parts, "fsdp", scatter_dimension=0, tiled=False)
+    index = lax.axis_index("fsdp")
+    half = parts.shape[1] // 2
+
+    def part(bits):
+        return lax.dynamic_index_in_dim(parts, index ^ bits, 0, keepdims=False)
+
+    corner, far, near = part(3), part(2), part(1)
+    from_near = cross(corner[:half], 1)
+    from_far = cross(corner[half:], 2)
+    far = jnp.concatenate([add(far[:half], from_near), far[half:]], axis=0)
+    near = jnp.concatenate([near[:half], add(near[half:], from_far)], axis=0)
+    total = part(0).astype(f32) + cross(near, 1).astype(f32) + cross(far, 2).astype(f32)
+    return total.astype(parts.dtype)
+
+
+def sum_ctx(value):
+    if lax.axis_size("ctx") != 4:
+        return lax.psum(value, "ctx")
+    index = lax.axis_index("ctx")
+    inner = (index == 1) | (index == 2)
+    value = add(value, lax.ppermute(value, "ctx", [(0, 1), (3, 2)]))
+    value = add(value, lax.ppermute(value, "ctx", [(1, 2), (2, 1)]))
+    return jnp.where(inner, value, lax.ppermute(value, "ctx", [(1, 0), (2, 3)]))
 
 
 def shards(
@@ -261,7 +325,7 @@
     pack = jnp.concatenate(
         [ln_gain[0], ln_bias[0], attn_bias[0], out_bias[0], fc_bias[0].reshape(-1, shard_width)]
     )
-    pack = lax.all_gather(pack, "fsdp", axis=0)
+    pack = gather_fsdp(pack)
     packs = trade(pack)
 
     def unpack(packed):
@@ -281,11 +345,14 @@
     pieces = [halves(matrix[0]) for matrix in (w_qkv, w_proj, w_fc, w_out)]
 
     def whole_weight(piece):
-        gathered = lax.all_gather(piece, "fsdp", axis=0)
-        low, high = trade(gathered)
+        low, high = trade(gather_fsdp(piece))
         return jnp.stack([low, high], axis=1).reshape(-1, piece.shape[-1])
 
-    weights = [tuple(whole_weight(piece[layer]) for piece in pieces) for layer in range(2)]
+    weights_zero = tuple(whole_weight(piece[0]) for piece in pieces)
+    later = tuple(piece[1] for piece in pieces)
+    w_qkv_zero, later = lax.optimization_barrier((weights_zero[0], later))
+    weights_zero = (w_qkv_zero, *weights_zero[1:])
+    weights = [weights_zero, tuple(whole_weight(piece) for piece in later)]
 
     def own(padded):
         return lax.dynamic_slice_in_dim(padded, section * (ctxs * per), ctxs * per, 0)
@@ -300,6 +367,9 @@
     places = lax.dynamic_index_in_dim(places, ctx_index, 0, keepdims=False)
     order = (
         lax.broadcasted_iota(jnp.int32, (per, length, length), 1) == places[:, None, :]
+    ).astype(bf16)
+    order_back = (
+        lax.broadcasted_iota(jnp.int32, (per, length, length), 2) == places[:, :, None]
     ).astype(bf16)
 
     def to_sorted(rows):
@@ -309,42 +379,44 @@
             .reshape(per * length, width)
         )
 
-    def to_stored(rows):
-        return jnp.einsum(
-            "bpt,bpd->btd", order, rows.reshape(per, length, width), preferred_element_type=f32
+    def spread(rows):
+        stored = jnp.einsum(
+            "btp,bpd->btd", order_back, rows.reshape(per, length, width), preferred_element_type=f32
         ).astype(bf16)
+        cut = stored.reshape(per, ctxs, local_rows, width)
+        moved = lax.all_to_all(cut, "ctx", 1, 1, tiled=True)
+        return jnp.transpose(moved, (1, 0, 2, 3)).reshape(ctxs * per, local_rows, width)
 
     def home(zero, one):
         arrived = swap(jnp.where(first, one, zero))
         mine = jnp.where(first, zero, one)
-        both = jnp.stack([jnp.where(first, mine, arrived), jnp.where(first, arrived, mine)])
-        both = both.reshape(sections, per, ctxs, local_rows, width)
-        moved = lax.all_to_all(both, "ctx", 2, 2, tiled=True)
-        ordered = jnp.transpose(moved, (0, 2, 1, 3, 4)).reshape(slots, local_rows, width)
-        return ordered[:local_seqs][None]
+        low, high = jnp.where(first, mine, arrived), jnp.where(first, arrived, mine)
+        return jnp.concatenate([low, high], axis=0)[:local_seqs][None]
 
     start = to_sorted(bring(block_input))
     grad_final = to_sorted(bring(cotangent))
     middle, kept_zero = layer_forward(weights[0], smalls[0], start, length)
     final, kept_one = layer_forward(weights[1], smalls[1], middle, length)
-    section_out = home(to_stored(middle), to_stored(final))
+    out_zero = spread(middle)
+    out_one = spread(final)
 
     def send(grad):
         cut = grad.reshape(fsdps, 2, -1, grad.shape[-1])
         low, high = cut[:, 0], cut[:, 1]
         arrived = swap(jnp.where(first, high, low))
         mine = jnp.where(first, low, high)
-        both = (mine.astype(f32) + arrived.astype(f32)).astype(bf16)
-        scattered = lax.psum_scatter(both, "fsdp", scatter_dimension=0, tiled=False)
-        return lax.psum(scattered, "ctx")
+        return sum_ctx(scatter_fsdp(add(mine, arrived)))
 
     grad_middle, grads_one, small_one = layer_back(
         weights[1], smalls[1], kept_one, grad_final, length, send
     )
+    grad_middle, out_zero, out_one = lax.optimization_barrier((grad_middle, out_zero, out_one))
+    in_one = spread(grad_middle)
     grad_start, grads_zero, small_zero = layer_back(
         weights[0], smalls[0], kept_zero, grad_middle, length, send
     )
-    section_in_grad = home(to_stored(grad_start), to_stored(grad_middle))
+    section_out = home(out_zero, out_one)
+    section_in_grad = home(spread(grad_start), in_one)
 
     def finish(zero, one):
         arrived = swap(jnp.where(first, one, zero))
@@ -360,10 +432,9 @@
         vectors = jnp.transpose(vectors.reshape(8, fsdps, shard_width), (1, 0, 2))
         return jnp.concatenate([vectors, fc.reshape(fsdps, -1, shard_width)], axis=1)
 
-    packed = jnp.stack([repack(small_zero), repack(small_one)])
-    packed = lax.psum(packed, ("section", "ctx", "fsdp"))
-    packed = lax.dynamic_index_in_dim(packed, section, 0, keepdims=False)
-    packed = lax.dynamic_index_in_dim(packed, lax.axis_index("fsdp"), 0, keepdims=False)
+    pack_zero, pack_one = repack(small_zero), repack(small_one)
+    arrived = swap(jnp.where(first, pack_one, pack_zero))
+    packed = sum_ctx(scatter_fsdp(jnp.where(first, pack_zero, pack_one) + arrived))
     return (
         section_out,
         section_in_grad,

time: 1090 us -> 1000 us (0.917)
  waiting for transfers between devices: 515 us -> 322 us
  starting transfers between devices: 27.8 us -> 169 us
  blocking collectives: 36.5 us -> 0 us
  other arithmetic: 109 us -> 137 us
  matrix products: 205 us -> 192 us
  between operations: 16.5 us -> 4.36 us
    psum x2 -> x0, waiting for transfers between devices: 257 us -> none  [the longest x1 128 us: shards(): packed = lax.psum(packed, ('section', 'ctx', 'fsdp'))]
    ppermute x0 -> x99, waiting for transfers between devices: none -> 242 us  [the longest x72 135 us: cross(): return lax.ppermute(value, 'fsdp', [(i, i ^ bit) for i in range(4)])]
    ppermute x0 -> x99, starting transfers between devices: none -> 136 us  [the longest x72 76.3 us: cross(): return lax.ppermute(value, 'fsdp', [(i, i ^ bit) for i in range(4)])]
    all_gather x6 -> x0, waiting for transfers between devices: 134 us -> none  [whole_weight(): gathered = lax.all_gather(piece, 'fsdp', axis=0)]
    unnamed x24 -> x0, waiting for transfers between devices: 38.4 us -> none
    all_gather x3 -> x0, blocking collectives: 36.5 us -> none  [the longest x2 28.3 us: whole_weight(): gathered = lax.all_gather(piece, 'fsdp', axis=0)]
    ppermute x27 -> x28, waiting for transfers between devices: 15.8 us -> 1.06 us  [swap(): return lax.ppermute(value, 'section', [(0, 1), (1, 0)])]
    convert_element_type x8 -> x41, other arithmetic: 28.2 us -> 41.6 us  [the longest x32 34.5 us: add(): return (left.astype(f32) + right.astype(f32)).astype(left.dtype)]
  transfers between devices with their start and end apart: 47 -> 133, of which waited for: 16 -> 51; matrix products, arithmetic and copies ran while one was open for 24% -> 38% of each run, Pallas kernels for 5% -> 10%
where the time goes in v2:
time: 1000 us; the launch traced here: 993 us
  waiting for transfers between devices  322 us (32%)
  matrix products  192 us (19%)
  starting transfers between devices  169 us (17%)
  other arithmetic  137 us (14%)
  Pallas kernels  99.1 us (10%)
  local copies, waits for them, and re-layouts  70.3 us (7%)
    ppermute x72, waiting for transfers between devices, cross(): return lax.ppermute(value, 'fsdp', [(i, i ^ bit) for i in range(4)])  135 us
    ppermute x72, starting transfers between devices, cross(): return lax.ppermute(value, 'fsdp', [(i, i ^ bit) for i in range(4)])  76.3 us
    dot_general x8, matrix products, mm_tn(): lax.dot_general(left, right, (((0,), (0,)), ((), ())), preferred_element_...  61.7 us
    dot_general x8, matrix products, mm_nt(): lax.dot_general(left, right, (((1,), (1,)), ((), ())), preferred_element_...  55.5 us
    ppermute x9, waiting for transfers between devices, sum_ctx(): value = add(value, lax.ppermute(value, 'ctx', [(0, 1), (3, 2)]))  54.3 us
    ppermute x9, waiting for transfers between devices, sum_ctx(): return jnp.where(inner, value, lax.ppermute(value, 'ctx', [(1, 0), (2, 3)]))  53.1 us
    all_to_all x4, waiting for transfers between devices, spread(): moved = lax.all_to_all(cut, 'ctx', 1, 1, tiled=True)  53.1 us
    pallas_call x2, Pallas kernels, attend_back(): pl.pallas_call(functools.partial(attend_back_kernel, query_block(length))...  51.7 us
  transfers between devices with their start and end apart: 133, of which 51 were waited for; matrix products, arithmetic and copies ran while one was open for 38% of the time, Pallas kernels for 10%

profile of v2, /device:TPU:0, one launch (start us, length us, event | category | flops | bytes accessed | tf_op | source)
XLA Modules:
  0.0 993.4 jit_solution(4763440344351823688)
XLA Ops:
  15.0 5.0 all-to-all-start.1
  73.8 4.9 collective-permute-done.7
  83.0 25.8 %collective-permute-done.8 = bf16[48,2304]{1,0:T(8,128)(2,1)S(1)} collective-permute-done((bf16[48,2304]{1,0:T(8,128)(2,1)S(1)}, bf16[48,2304]{1,0:T(8,128)(2,1)S(1)}, u32[]{:S(2)}, u32[]{:S(2)}) %collective-permute-start.8) | collective-permute-done | bytes 221216 | tf_op jit(solution)/shard_map/ppermute | solution.py:243
  110.1 5.4 collective-permute-done.9
  123.3 5.4 collective-permute-done.22
  128.7 5.5 all-to-all-start
  144.9 26.0 %all-to-all-done = bf16[4,1,256,768]{3,2,1,0:T(8,128)(2,1)} async-done(((bf16[4,1,256,768]{3,2,1,0:T(8,128)(2,1)}), bf16[4,1,256,768]{3,2,1,0:T(8,128)(2,1)}, u32[]{:S(2)}, u32[]{:S(2)}) %all-to-all-start) | async-done | bytes 1572896 | tf_op jit(solution)/shard_map/all_to_all | solution.py:363
  183.0 4.5 add_convert_fusion.1.q_ref.k_ref.v_ref
  187.6 24.0 %shard_map.203 = (bf16[1024,768]{1,0:T(8,128)(2,1)S(1)}, f32[1,6,2,1024]{3,2,1,0:T(2,128)S(1)}) custom-call(bf16[1024,2304]{1,0:T(8,128)(2,1)S(1)} %add_convert_fusion.1.q_ref.k_ref.v_ref, bf16[1024,2304]{1,0:T(8,128)(2,1)S(1)} %add_convert_fusion.1.q_ref.k_ref.v_ref, bf16[1024,2304]{1,0:T(8,128)(2,1)S(1)} %add_convert_fusion.1.q_ref.k_ref.v_ref), custom_call_target="tpu_custom_call" | custom-call | flops 6442450944 | bytes 6291456 | tf_op jit(solution)/shard_map/pallas_call | solution.py:116
  215.2 3.8 collective-permute-done.36
  222.7 12.5 %collective-permute-done.44 = bf16[384,768]{1,0:T(8,128)(2,1)S(1)} collective-permute-done((bf16[384,768]{1,0:T(8,128)(2,1)S(1)}, bf16[384,768]{1,0:T(8,128)(2,1)S(1)}, u32[]{:S(2)}, u32[]{:S(2)}) %collective-permute-start.44) | collective-permute-done | bytes 589856 | tf_op jit(solution)/shard_map/ppermute | solution.py:243
  235.9 9.9 collective-permute-done.39
  271.9 8.2 fusion.136
  280.2 11.0 %convert_reduce_fusion.2 = (f32[1024]{0:T(1024)S(1)}, bf16[1024,768]{1,0:T(8,128)(2,1)S(1)}) fusion(f32[768]{0:T(1024)S(1)} %copy-done.155, f32[1024,768]{1,0:T(8,128)S(1)} %get-tuple-element.266, bf16[3072,768]{1,0:T(8,128)(2,1)S(1)} %bitcast.642, f32[1024,3072]{1,0:T(8,128)} %fusion.136, f32[3072]{0:T(1024)S(1)} %copy-done.142), kind=kOutput, calls=%fused_computation.36 | convolution fusion | flops 4867226624 | bytes 22039552 | tf_op jit(solution)/shard_map/dot_general | solution.py:32
  294.3 4.5 all-to-all-start.2
  304.1 4.5 add_convert_fusion.q_ref.k_ref.v_ref
  308.7 23.5 %shard_map.204 = (bf16[1024,768]{1,0:T(8,128)(2,1)S(1)}, f32[1,6,2,1024]{3,2,1,0:T(2,128)S(1)}) custom-call(bf16[1024,2304]{1,0:T(8,128)(2,1)S(1)} %add_convert_fusion.q_ref.k_ref.v_ref, bf16[1024,2304]{1,0:T(8,128)(2,1)S(1)} %add_convert_fusion.q_ref.k_ref.v_ref, bf16[1024,2304]{1,0:T(8,128)(2,1)S(1)} %add_convert_fusion.q_ref.k_ref.v_ref), custom_call_target="tpu_custom_call" | custom-call | flops 6442450944 | bytes 6291456 | tf_op jit(solution)/shard_map/pallas_call | solution.py:116
  344.5 8.5 fusion.137
  353.1 12.1 %convolution_convert_fusion.3 = bf16[3072,768]{1,0:T(8,128)(2,1)} fusion(bf16[1024,768]{1,0:T(8,128)(2,1)S(1)} %fusion.63, f32[1024,3072]{1,0:T(8,128)} %fusion.137, f32[3072]{0:T(1024)S(1)} %copy-done.144), kind=kOutput, calls=%fused_computation.27 | convolution fusion | flops 4865654784 | bytes 18886656 | tf_op jit(solution)/shard_map/dot_general | solution.py:40
  365.2 16.4 %fusion.13 = bf16[1024,3072]{1,0:T(8,128)(2,1)} fusion(f32[1024,3072]{1,0:T(8,128)} %fusion.137, f32[3072]{0:T(1024)S(1)} %copy-done.144, bf16[1024,768]{1,0:T(8,128)(2,1)S(1)} %fusion.63, bf16[3072,768]{1,0:T(8,128)(2,1)} %bitcast.644), kind=kOutput, calls=%fused_computation.17 | convolution fusion | flops 4897898496 | bytes 25178112 | tf_op jit(solution)/shard_map/dot_general | solution.py:36
  381.6 10.5 %convolution_convert_fusion.2 = bf16[768,3072]{1,0:T(8,128)(2,1)} fusion(bf16[1024,3072]{1,0:T(8,128)(2,1)} %fusion.13, f32[1024,768]{1,0:T(8,128)S(1)} %get-tuple-element.270, f32[768]{0:T(1024)S(1)} %copy-done.153, f32[768]{0:T(1024)S(1)} %copy-done.139, f32[1024]{0:T(1024)S(1)} %fusion.129, f32[1024]{0:T(1024)S(1)} %broadcast_multiply_fusion), kind=kOutput, calls=%fused_computation.26 | convolution fusion | flops 4838129664 | bytes 14170112 | tf_op jit(solution)/shard_map/dot_general | solution.py:40
  392.1 8.0 multiply_reduce_fusion
  407.2 25.7 %shard_map.205 = (bf16[1024,768]{1,0:T(8,128)(2,1)S(1)}, bf16[1024,768]{1,0:T(8,128)(2,1)S(1)}, bf16[1024,768]{1,0:T(8,128)(2,1)S(1)}) custom-call(bf16[1024,2304]{1,0:T(8,128)(2,1)S(1)} %add_convert_fusion.q_ref.k_ref.v_ref, bf16[1024,2304]{1,0:T(8,128)(2,1)S(1)} %add_convert_fusion.q_ref.k_ref.v_ref, ...), custom_call_target="tpu_custom_call" | custom-call | flops 16106127360 | bytes 12582912 | tf_op jit(solution)/shard_map/pallas_call | solution.py:138
  435.5 17.0 %fusion.70 = bf16[1024,768]{1,0:T(8,128)(2,1)} fusion(s32[1024]{0:T(1024)S(1)} %bitcast.665, f32[1024,768]{1,0:T(8,128)} %copy-done.16, bf16[3072,768]{1,0:T(8,128)(2,1)} %bitcast.645, f32[768]{0:T(1024)S(1)} %copy-done.152, f32[1024,3072]{1,0:T(8,128)} %fusion.137, f32[3072]{0:T(1024)S(1)} %copy-done.144), kind=kOutput, calls=%fused_computation.166 | convolution fusion | flops 6478102528 | bytes 22039552 | tf_op jit(solution)/shard_map/btp,bpd->btd/dot_general | solution.py:383
  455.1 7.1 convolution_convert_fusion.5
  462.3 4.1 fusion.139
  489.3 3.9 collective-permute-start.81
  493.2 4.0 select_bitcast_fusion.2
  498.7 4.3 all-to-all-start.3
  518.4 21.7 %all-to-all-done.3 = bf16[1,4,256,768]{3,2,0,1:T(8,128)(2,1)S(1)} async-done(((bf16[1,4,256,768]{3,2,0,1:T(8,128)(2,1)}), bf16[1,4,256,768]{3,2,0,1:T(8,128)(2,1)S(1)}, u32[]{:S(2)}, u32[]{:S(2)}) %all-to-all-start.3) | async-done | bytes 1572896 | tf_op jit(solution)/shard_map/all_to_all | solution.py:387
  540.2 13.3 %convolution_convert_fusion.1 = bf16[3072,768]{1,0:T(8,128)(2,1)} fusion(bf16[1024,768]{1,0:T(8,128)(2,1)S(1)} %copy-done.35, f32[1024,3072]{1,0:T(8,128)} %fusion.136, f32[3072]{0:T(1024)S(1)} %copy-done.143), kind=kOutput, calls=%fused_computation.25 | convolution fusion | flops 4865654784 | bytes 18886656 | tf_op jit(solution)/shard_map/dot_general | solution.py:40
  553.6 14.4 %fusion.6 = bf16[1024,3072]{1,0:T(8,128)(2,1)S(1)} fusion(f32[1024,3072]{1,0:T(8,128)} %fusion.136, f32[3072]{0:T(1024)S(1)} %copy-done.143, bf16[1024,768]{1,0:T(8,128)(2,1)S(1)} %copy-done.35, bf16[3072,768]{1,0:T(8,128)(2,1)} %bitcast.643), kind=kOutput, calls=%fused_computation.10 | convolution fusion | flops 4897898496 | bytes 25178112 | tf_op jit(solution)/shard_map/dot_general | solution.py:36
  568.0 8.1 convolution_convert_fusion
  576.1 5.7 multiply_reduce_fusion.1
  589.8 25.9 %shard_map.206 = (bf16[1024,768]{1,0:T(8,128)(2,1)S(1)}, bf16[1024,768]{1,0:T(8,128)(2,1)S(1)}, bf16[1024,768]{1,0:T(8,128)(2,1)S(1)}) custom-call(bf16[1024,2304]{1,0:T(8,128)(2,1)S(1)} %bitcast.607, bf16[1024,2304]{1,0:T(8,128)(2,1)S(1)} %bitcast.607, bf16[1024,2304]{1,0:T(8,128)(2,1)S(1)} %bitcast.607, ...), custom_call_target="tpu_custom_call" | custom-call | flops 16106127360 | bytes 12582912 | tf_op jit(solution)/shard_map/pallas_call | solution.py:138
  617.3 5.6 convolution_convert_fusion.4
  622.9 4.1 fusion.138
  631.7 3.8 convert_reduce_fusion.1
  649.5 4.4 fusion.71
  661.5 4.0 fusion.22
  670.7 3.9 collective-permute-start.124
  676.0 9.9 %collective-permute-done.124 = f32[12,192]{1,0:T(8,128)S(1)} collective-permute-done((f32[12,192]{1,0:T(8,128)S(1)}, f32[12,192]{1,0:T(8,128)S(1)}, u32[]{:S(2)}, u32[]{:S(2)}) %collective-permute-start.124) | collective-permute-done | bytes 9248 | tf_op jit(solution)/shard_map/ppermute | solution.py:289
  693.5 9.8 collective-permute-done.126
  705.1 5.3 collective-permute-done.96
  712.9 4.5 collective-permute-start.64
  736.4 8.0 collective-permute-done.95
  747.8 6.2 collective-permute-done.112
  757.2 5.4 collective-permute-done.75
  767.6 7.4 collective-permute-done.98
  775.0 4.4 collective-permute-start.115
  780.4 9.0 collective-permute-done.115
  803.0 7.6 all-to-all-start.5
  818.6 4.0 fusion.23
  824.3 4.3 fusion.25
  828.6 31.3 %all-to-all-done.5 = bf16[1,4,256,768]{3,2,0,1:T(8,128)(2,1)S(1)} async-done(((bf16[1,4,256,768]{3,2,0,1:T(8,128)(2,1)}), bf16[1,4,256,768]{3,2,0,1:T(8,128)(2,1)S(1)}, u32[]{:S(2)}, u32[]{:S(2)}) %all-to-all-start.5) | async-done | bytes 1572896 | tf_op jit(solution)/shard_map/all_to_all | solution.py:387
  866.4 4.0 collective-permute-done.105
  870.4 9.0 collective-permute-start.56
  887.5 9.5 collective-permute-done.87
  902.8 4.0 collective-permute-done.106
  907.1 9.4 collective-permute-start.107
  919.0 11.1 %collective-permute-done.107 = bf16[384,768]{1,0:T(8,128)(2,1)S(1)} collective-permute-done((bf16[384,768]{1,0:T(8,128)(2,1)S(1)}, bf16[384,768]{1,0:T(8,128)(2,1)S(1)}, u32[]{:S(2)}, u32[]{:S(2)}) %collective-permute-start.107) | collective-permute-done | bytes 589856 | tf_op jit(solution)/shard_map/ppermute | solution.py:289
  930.2 12.1 %collective-permute-done.90 = bf16[96,3072]{1,0:T(8,128)(2,1)S(1)} collective-permute-done((bf16[96,3072]{1,0:T(8,128)(2,1)S(1)}, bf16[96,3072]{1,0:T(8,128)(2,1)S(1)}, u32[]{:S(2)}, u32[]{:S(2)}) %collective-permute-start.90) | collective-permute-done | bytes 589856 | tf_op jit(solution)/shard_map/ppermute | solution.py:289
  948.8 26.6 %collective-permute-done.109 = bf16[384,768]{1,0:T(8,128)(2,1)S(1)} collective-permute-done((bf16[384,768]{1,0:T(8,128)(2,1)S(1)}, bf16[384,768]{1,0:T(8,128)(2,1)S(1)}, u32[]{:S(2)}, u32[]{:S(2)}) %collective-permute-start.109) | collective-permute-done | bytes 589856 | tf_op jit(solution)/shard_map/ppermute | solution.py:291
  976.7 11.3 %collective-permute-done.92 = bf16[96,3072]{1,0:T(8,128)(2,1)S(1)} collective-permute-done((bf16[96,3072]{1,0:T(8,128)(2,1)S(1)}, bf16[96,3072]{1,0:T(8,128)(2,1)S(1)}, u32[]{:S(2)}, u32[]{:S(2)}) %collective-permute-start.92) | collective-permute-done | bytes 589856 | tf_op jit(solution)/shard_map/ppermute | solution.py:291
  (864 shorter events, 353.8 us)
Async XLA Ops:
  2.3 18.4 %collective-permute-start.1 = (bf16[12,192]{1,0:T(8,128)(2,1)S(1)}, bf16[12,192]{1,0:T(8,128)(2,1)S(1)}, u32[]{:S(2)}, u32[]{:S(2)}) collective-permute-start(bf16[12,192]{1,0:T(8,128)(2,1)S(1)} %concatenate.166), channel_id=1, source_target_pairs={{0,2},{1,3},{2,0},{3,1},{4,6},{5,7},{6,4},{7,5},{8,10},{9,11},{10,... | collective-permute-start | bytes 13832 | tf_op jit(solution)/shard_map/ppermute | solution.py:243
  8.8 55.1 %collective-permute-start.5 = (bf16[96,2304]{1,0:T(8,128)(2,1)}, bf16[96,2304]{1,0:T(8,128)(2,1)}, u32[]{:S(2)}, u32[]{:S(2)}) collective-permute-start(bf16[96,2304]{1,0:T(8,128)(2,1)} %select_bitcast_fusion.56), channel_id=1, source_target_pairs={{0,16},{16,0},{1,17},{17,1},{2,18},{18,2},{3,19},{19,3},{4,20},{20... | collective-permute-start | bytes 1327112 | tf_op jit(solution)/shard_map/ppermute | solution.py:239
  10.9 57.1 %collective-permute-start.12 = (bf16[96,3072]{1,0:T(8,128)(2,1)}, bf16[96,3072]{1,0:T(8,128)(2,1)}, u32[]{:S(2)}, u32[]{:S(2)}) collective-permute-start(bf16[96,3072]{1,0:T(8,128)(2,1)} %select_bitcast_fusion.45), channel_id=1, source_target_pairs={{0,16},{16,0},{1,17},{17,1},{2,18},{18,2},{3,19},{19,3},{4,20},{20... | collective-permute-start | bytes 1769480 | tf_op jit(solution)/shard_map/ppermute | solution.py:239
  12.3 59.0 %collective-permute-start.13 = (bf16[384,768]{1,0:T(8,128)(2,1)}, bf16[384,768]{1,0:T(8,128)(2,1)}, u32[]{:S(2)}, u32[]{:S(2)}) collective-permute-start(bf16[384,768]{1,0:T(8,128)(2,1)} %select_bitcast_fusion.44), channel_id=1, source_target_pairs={{0,16},{16,0},{1,17},{17,1},{2,18},{18,2},{3,19},{19,3},{4,20},{20... | collective-permute-start | bytes 1769480 | tf_op jit(solution)/shard_map/ppermute | solution.py:239
  15.0 113.7 %all-to-all-start.1 = ((bf16[4,1,256,768]{3,2,1,0:T(8,128)(2,1)}), bf16[4,1,256,768]{3,2,1,0:T(8,128)(2,1)}, u32[]{:S(2)}, u32[]{:S(2)}) async-start(bf16[4,1,256,768]{3,2,1,0:T(8,128)(2,1)} %fusion.74), calls=%async_computation.1 | async-start | bytes 3145728 | tf_op jit(solution)/shard_map/all_to_all | solution.py:363
  28.6 27.7 %collective-permute-start.15 = (bf16[96,768]{1,0:T(8,128)(2,1)}, bf16[96,768]{1,0:T(8,128)(2,1)S(1)}, u32[]{:S(2)}, u32[]{:S(2)}) collective-permute-start(bf16[96,768]{1,0:T(8,128)(2,1)} %get-tuple-element.243), channel_id=1, source_target_pairs={{0,2},{1,3},{2,0},{3,1},{4,6},{5,7},{6,4},{7,5},{8,10},{9,11},{10,... | collective-permute-start | bytes 442376 | tf_op jit(solution)/shard_map/ppermute | solution.py:243
  30.6 27.6 %collective-permute-start.14 = (bf16[96,768]{1,0:T(8,128)(2,1)}, bf16[96,768]{1,0:T(8,128)(2,1)S(1)}, u32[]{:S(2)}, u32[]{:S(2)}) collective-permute-start(bf16[96,768]{1,0:T(8,128)(2,1)} %get-tuple-element.243), channel_id=1, source_target_pairs={{0,1},{1,0},{2,3},{3,2},{4,5},{5,4},{6,7},{7,6},{8,9},{9,8},{10,11... | collective-permute-start | bytes 442376 | tf_op jit(solution)/shard_map/ppermute | solution.py:243
  63.8 17.3 %collective-permute-start.18 = (bf16[4,96,768]{2,1,0:T(8,128)(2,1)S(1)}, bf16[4,96,768]{2,1,0:T(8,128)(2,1)S(1)}, u32[]{:S(2)}, u32[]{:S(2)}) collective-permute-start(bf16[4,96,768]{2,1,0:T(8,128)(2,1)S(1)} %pad_maximum_fusion.16), channel_id=1, source_target_pairs={{0,16},{16,0},{1,17},{17,1},{2,18},{18,2},{3,19},{19,3},{4,20},{20... | collective-permute-start | bytes 1769480 | tf_op jit(solution)/shard_map/ppermute | solution.py:239
  70.0 45.7 %collective-permute-start.20 = (bf16[96,3072]{1,0:T(8,128)(2,1)S(1)}, bf16[96,3072]{1,0:T(8,128)(2,1)S(1)}, u32[]{:S(2)}, u32[]{:S(2)}) collective-permute-start(bf16[96,3072]{1,0:T(8,128)(2,1)S(1)} %get-tuple-element.201), channel_id=1, source_target_pairs={{0,2},{1,3},{2,0},{3,1},{4,6},{5,7},{6,4},{7,5},{8,10},{9,11},{10,... | collective-permute-start | bytes 1769480 | tf_op jit(solution)/shard_map/ppermute | solution.py:243
  71.3 47.5 %collective-permute-start.19 = (bf16[96,3072]{1,0:T(8,128)(2,1)S(1)}, bf16[96,3072]{1,0:T(8,128)(2,1)S(1)}, u32[]{:S(2)}, u32[]{:S(2)}) collective-permute-start(bf16[96,3072]{1,0:T(8,128)(2,1)S(1)} %get-tuple-element.201), channel_id=1, source_target_pairs={{0,1},{1,0},{2,3},{3,2},{4,5},{5,4},{6,7},{7,6},{8,9},{9,8},{10,11... | collective-permute-start | bytes 1769480 | tf_op jit(solution)/shard_map/ppermute | solution.py:243
  78.7 41.5 %collective-permute-start.25 = (bf16[384,768]{1,0:T(8,128)(2,1)S(1)}, bf16[384,768]{1,0:T(8,128)(2,1)S(1)}, u32[]{:S(2)}, u32[]{:S(2)}) collective-permute-start(bf16[384,768]{1,0:T(8,128)(2,1)S(1)} %get-tuple-element.203), channel_id=1, source_target_pairs={{0,2},{1,3},{2,0},{3,1},{4,6},{5,7},{6,4},{7,5},{8,10},{9,11},{10,... | collective-permute-start | bytes 1769480 | tf_op jit(solution)/shard_map/ppermute | solution.py:243
  79.5 42.0 %collective-permute-start.24 = (bf16[384,768]{1,0:T(8,128)(2,1)S(1)}, bf16[384,768]{1,0:T(8,128)(2,1)S(1)}, u32[]{:S(2)}, u32[]{:S(2)}) collective-permute-start(bf16[384,768]{1,0:T(8,128)(2,1)S(1)} %get-tuple-element.203), channel_id=1, source_target_pairs={{0,1},{1,0},{2,3},{3,2},{4,5},{5,4},{6,7},{7,6},{8,9},{9,8},{10,11... | collective-permute-start | bytes 1769480 | tf_op jit(solution)/shard_map/ppermute | solution.py:243
  81.1 27.7 %collective-permute-start.8 = (bf16[48,2304]{1,0:T(8,128)(2,1)S(1)}, bf16[48,2304]{1,0:T(8,128)(2,1)S(1)}, u32[]{:S(2)}, u32[]{:S(2)}) collective-permute-start(bf16[48,2304]{1,0:T(8,128)(2,1)S(1)} %slice.717), channel_id=1, source_target_pairs={{0,1},{1,0},{2,3},{3,2},{4,5},{5,4},{6,7},{7,6},{8,9},{9,8},{10,11... | collective-permute-start | bytes 663560 | tf_op jit(solution)/shard_map/ppermute | solution.py:243
  118.8 55.6 %collective-permute-start.10 = (bf16[4,96,2304]{2,1,0:T(8,128)(2,1)}, bf16[4,96,2304]{2,1,0:T(8,128)(2,1)}, u32[]{:S(2)}, u32[]{:S(2)}) collective-permute-start(bf16[4,96,2304]{2,1,0:T(8,128)(2,1)} %pad_maximum_fusion.12), channel_id=1, source_target_pairs={{0,16},{16,0},{1,17},{17,1},{2,18},{18,2},{3,19},{19,3},{4,20},{20... | collective-permute-start | bytes 5308424 | tf_op jit(solution)/shard_map/ppermute | solution.py:239
  128.7 42.1 %all-to-all-start = ((bf16[4,1,256,768]{3,2,1,0:T(8,128)(2,1)}), bf16[4,1,256,768]{3,2,1,0:T(8,128)(2,1)}, u32[]{:S(2)}, u32[]{:S(2)}) async-start(bf16[4,1,256,768]{3,2,1,0:T(8,128)(2,1)} %fusion.73), calls=%async_computation | async-start | bytes 3145728 | tf_op jit(solution)/shard_map/all_to_all | solution.py:363
  177.6 36.1 %collective-permute-start.35 = (bf16[96,768]{1,0:T(8,128)(2,1)S(1)}, bf16[96,768]{1,0:T(8,128)(2,1)S(1)}, u32[]{:S(2)}, u32[]{:S(2)}) collective-permute-start(bf16[96,768]{1,0:T(8,128)(2,1)S(1)} %copy-done.118), channel_id=1, source_target_pairs={{0,2},{1,3},{2,0},{3,1},{4,6},{5,7},{6,4},{7,5},{8,10},{9,11},{10,... | collective-permute-start | bytes 442376 | tf_op jit(solution)/shard_map/ppermute | solution.py:243
  178.9 35.5 %collective-permute-start.34 = (bf16[96,768]{1,0:T(8,128)(2,1)S(1)}, bf16[96,768]{1,0:T(8,128)(2,1)S(1)}, u32[]{:S(2)}, u32[]{:S(2)}) collective-permute-start(bf16[96,768]{1,0:T(8,128)(2,1)S(1)} %copy-done.118), channel_id=1, source_target_pairs={{0,1},{1,0},{2,3},{3,2},{4,5},{5,4},{6,7},{7,6},{8,9},{9,8},{10,11... | collective-permute-start | bytes 442376 | tf_op jit(solution)/shard_map/ppermute | solution.py:243
  179.5 40.8 %collective-permute-start.30 = (bf16[96,2304]{1,0:T(8,128)(2,1)S(1)}, bf16[96,2304]{1,0:T(8,128)(2,1)S(1)}, u32[]{:S(2)}, u32[]{:S(2)}) collective-permute-start(bf16[96,2304]{1,0:T(8,128)(2,1)S(1)} %copy-done.104), channel_id=1, source_target_pairs={{0,2},{1,3},{2,0},{3,1},{4,6},{5,7},{6,4},{7,5},{8,10},{9,11},{10,... | collective-permute-start | bytes 1327112 | tf_op jit(solution)/shard_map/ppermute | solution.py:243
  180.2 41.6 %collective-permute-start.29 = (bf16[96,2304]{1,0:T(8,128)(2,1)S(1)}, bf16[96,2304]{1,0:T(8,128)(2,1)S(1)}, u32[]{:S(2)}, u32[]{:S(2)}) collective-permute-start(bf16[96,2304]{1,0:T(8,128)(2,1)S(1)} %copy-done.104), channel_id=1, source_target_pairs={{0,1},{1,0},{2,3},{3,2},{4,5},{5,4},{6,7},{7,6},{8,9},{9,8},{10,11... | collective-permute-start | bytes 1327112 | tf_op jit(solution)/shard_map/ppermute | solution.py:243
  181.7 40.9 %collective-permute-start.45 = (bf16[384,768]{1,0:T(8,128)(2,1)S(1)}, bf16[384,768]{1,0:T(8,128)(2,1)S(1)}, u32[]{:S(2)}, u32[]{:S(2)}) collective-permute-start(bf16[384,768]{1,0:T(8,128)(2,1)S(1)} %copy-done.98), channel_id=1, source_target_pairs={{0,2},{1,3},{2,0},{3,1},{4,6},{5,7},{6,4},{7,5},{8,10},{9,11},{10,... | collective-permute-start | bytes 1769480 | tf_op jit(solution)/shard_map/ppermute | solution.py:243
  219.0 16.3 %collective-permute-start.44 = (bf16[384,768]{1,0:T(8,128)(2,1)S(1)}, bf16[384,768]{1,0:T(8,128)(2,1)S(1)}, u32[]{:S(2)}, u32[]{:S(2)}) collective-permute-start(bf16[384,768]{1,0:T(8,128)(2,1)S(1)} %copy-done.98), channel_id=1, source_target_pairs={{0,1},{1,0},{2,3},{3,2},{4,5},{5,4},{6,7},{7,6},{8,9},{9,8},{10,11... | collective-permute-start | bytes 1769480 | tf_op jit(solution)/shard_map/ppermute | solution.py:243
  220.3 25.5 %collective-permute-start.39 = (bf16[96,3072]{1,0:T(8,128)(2,1)S(1)}, bf16[96,3072]{1,0:T(8,128)(2,1)S(1)}, u32[]{:S(2)}, u32[]{:S(2)}) collective-permute-start(bf16[96,3072]{1,0:T(8,128)(2,1)S(1)} %copy-done.97), channel_id=1, source_target_pairs={{0,1},{1,0},{2,3},{3,2},{4,5},{5,4},{6,7},{7,6},{8,9},{9,8},{10,11... | collective-permute-start | bytes 1769480 | tf_op jit(solution)/shard_map/ppermute | solution.py:243
  221.8 28.0 %collective-permute-start.31 = (bf16[48,2304]{1,0:T(8,128)(2,1)S(1)}, bf16[48,2304]{1,0:T(8,128)(2,1)S(1)}, u32[]{:S(2)}, u32[]{:S(2)}) collective-permute-start(bf16[48,2304]{1,0:T(8,128)(2,1)S(1)} %slice.735), channel_id=1, source_target_pairs={{0,1},{1,0},{2,3},{3,2},{4,5},{5,4},{6,7},{7,6},{8,9},{9,8},{10,11... | collective-permute-start | bytes 663560 | tf_op jit(solution)/shard_map/ppermute | solution.py:243
  222.6 43.9 %collective-permute-start.23 = (bf16[4,96,3072]{2,1,0:T(8,128)(2,1)S(1)}, bf16[4,96,3072]{2,1,0:T(8,128)(2,1)S(1)}, u32[]{:S(2)}, u32[]{:S(2)}) collective-permute-start(bf16[4,96,3072]{2,1,0:T(8,128)(2,1)S(1)} %copy-done.101), channel_id=1, source_target_pairs={{0,16},{16,0},{1,17},{17,1},{2,18},{18,2},{3,19},{19,3},{4,20},{20... | collective-permute-start | bytes 7077896 | tf_op jit(solution)/shard_map/ppermute | solution.py:239
  235.3 33.8 %collective-permute-start.28 = (bf16[4,384,768]{2,1,0:T(8,128)(2,1)S(1)}, bf16[4,384,768]{2,1,0:T(8,128)(2,1)S(1)}, u32[]{:S(2)}, u32[]{:S(2)}) collective-permute-start(bf16[4,384,768]{2,1,0:T(8,128)(2,1)S(1)} %copy-done.100), channel_id=1, source_target_pairs={{0,16},{16,0},{1,17},{17,1},{2,18},{18,2},{3,19},{19,3},{4,20},{20... | collective-permute-start | bytes 7077896 | tf_op jit(solution)/shard_map/ppermute | solution.py:239
  235.3 19.5 %collective-permute-start.38 = (bf16[4,96,768]{2,1,0:T(8,128)(2,1)S(1)}, bf16[4,96,768]{2,1,0:T(8,128)(2,1)S(1)}, u32[]{:S(2)}, u32[]{:S(2)}) collective-permute-start(bf16[4,96,768]{2,1,0:T(8,128)(2,1)S(1)} %pad_maximum_fusion.17), channel_id=1, source_target_pairs={{0,16},{16,0},{1,17},{17,1},{2,18},{18,2},{3,19},{19,3},{4,20},{20... | collective-permute-start | bytes 1769480 | tf_op jit(solution)/shard_map/ppermute | solution.py:239
  260.3 39.2 %collective-permute-start.33 = (bf16[4,96,2304]{2,1,0:T(8,128)(2,1)}, bf16[4,96,2304]{2,1,0:T(8,128)(2,1)}, u32[]{:S(2)}, u32[]{:S(2)}) collective-permute-start(bf16[4,96,2304]{2,1,0:T(8,128)(2,1)} %pad_maximum_fusion.13), channel_id=1, source_target_pairs={{0,16},{16,0},{1,17},{17,1},{2,18},{18,2},{3,19},{19,3},{4,20},{20... | collective-permute-start | bytes 5308424 | tf_op jit(solution)/shard_map/ppermute | solution.py:239
  262.5 71.9 %collective-permute-start.48 = (bf16[4,384,768]{2,1,0:T(8,128)(2,1)}, bf16[4,384,768]{2,1,0:T(8,128)(2,1)}, u32[]{:S(2)}, u32[]{:S(2)}) collective-permute-start(bf16[4,384,768]{2,1,0:T(8,128)(2,1)} %pad_maximum_fusion.11), channel_id=1, source_target_pairs={{0,16},{16,0},{1,17},{17,1},{2,18},{18,2},{3,19},{19,3},{4,20},{20... | collective-permute-start | bytes 7077896 | tf_op jit(solution)/shard_map/ppermute | solution.py:239
  266.5 74.9 %collective-permute-start.43 = (bf16[4,96,3072]{2,1,0:T(8,128)(2,1)}, bf16[4,96,3072]{2,1,0:T(8,128)(2,1)}, u32[]{:S(2)}, u32[]{:S(2)}) collective-permute-start(bf16[4,96,3072]{2,1,0:T(8,128)(2,1)} %pad_maximum_fusion.10), channel_id=1, source_target_pairs={{0,16},{16,0},{1,17},{17,1},{2,18},{18,2},{3,19},{19,3},{4,20},{20... | collective-permute-start | bytes 7077896 | tf_op jit(solution)/shard_map/ppermute | solution.py:239
  294.3 204.4 %all-to-all-start.2 = ((bf16[1,4,256,768]{3,2,0,1:T(8,128)(2,1)}), bf16[1,4,256,768]{3,2,0,1:T(8,128)(2,1)}, u32[]{:S(2)}, u32[]{:S(2)}) async-start(bf16[1,4,256,768]{3,2,0,1:T(8,128)(2,1)} %bitcast.653), calls=%async_computation.2 | async-start | bytes 3145728 | tf_op jit(solution)/shard_map/all_to_all | solution.py:387
  478.2 24.8 %collective-permute-start.59 = (bf16[4,96,2304]{2,1,0:T(8,128)(2,1)}, bf16[4,96,2304]{2,1,0:T(8,128)(2,1)}, u32[]{:S(2)}, u32[]{:S(2)}) collective-permute-start(bf16[4,96,2304]{2,1,0:T(8,128)(2,1)} %select_bitcast_fusion.12), channel_id=1, source_target_pairs={{0,16},{16,0},{1,17},{17,1},{2,18},{18,2},{3,19},{19,3},{4,20},{20... | collective-permute-start | bytes 5308424 | tf_op jit(solution)/shard_map/ppermute | solution.py:239
  484.5 175.5 %collective-permute-start.110 = (bf16[4,384,768]{2,1,0:T(8,128)(2,1)}, bf16[4,384,768]{2,1,0:T(8,128)(2,1)}, u32[]{:S(2)}, u32[]{:S(2)}) collective-permute-start(bf16[4,384,768]{2,1,0:T(8,128)(2,1)} %select_bitcast_fusion), channel_id=1, source_target_pairs={{0,16},{16,0},{1,17},{17,1},{2,18},{18,2},{3,19},{19,3},{4,20},{20... | collective-permute-start | bytes 7077896 | tf_op jit(solution)/shard_map/ppermute | solution.py:239
  497.2 141.7 %collective-permute-start.93 = (bf16[4,96,3072]{2,1,0:T(8,128)(2,1)}, bf16[4,96,3072]{2,1,0:T(8,128)(2,1)}, u32[]{:S(2)}, u32[]{:S(2)}) collective-permute-start(bf16[4,96,3072]{2,1,0:T(8,128)(2,1)} %select_bitcast_fusion.2), channel_id=1, source_target_pairs={{0,16},{16,0},{1,17},{17,1},{2,18},{18,2},{3,19},{19,3},{4,20},{20... | collective-permute-start | bytes 7077896 | tf_op jit(solution)/shard_map/ppermute | solution.py:239
  498.7 41.4 %all-to-all-start.3 = ((bf16[1,4,256,768]{3,2,0,1:T(8,128)(2,1)}), bf16[1,4,256,768]{3,2,0,1:T(8,128)(2,1)S(1)}, u32[]{:S(2)}, u32[]{:S(2)}) async-start(bf16[1,4,256,768]{3,2,0,1:T(8,128)(2,1)} %bitcast.88), calls=%async_computation.3 | async-start | bytes 3145728 | tf_op jit(solution)/shard_map/all_to_all | solution.py:387
  510.3 246.8 %collective-permute-start.83 = (bf16[96,768]{1,0:T(8,128)(2,1)}, bf16[96,768]{1,0:T(8,128)(2,1)}, u32[]{:S(2)}, u32[]{:S(2)}) collective-permute-start(bf16[96,768]{1,0:T(8,128)(2,1)} %add_convert_fusion.21), channel_id=1, source_target_pairs={{4,0},{8,12},{5,1},{9,13},{6,2},{10,14},{7,3},{11,15},{20,16},{24,... | collective-permute-start | bytes 442376 | tf_op jit(solution)/shard_map/ppermute | solution.py:291
  514.9 174.1 %collective-permute-start.61 = (bf16[96,2304]{1,0:T(8,128)(2,1)}, bf16[96,2304]{1,0:T(8,128)(2,1)}, u32[]{:S(2)}, u32[]{:S(2)}) collective-permute-start(bf16[96,2304]{1,0:T(8,128)(2,1)} %pad_maximum_fusion.28), channel_id=1, source_target_pairs={{0,1},{1,0},{2,3},{3,2},{4,5},{5,4},{6,7},{7,6},{8,9},{9,8},{10,11... | collective-permute-start | bytes 1327112 | tf_op jit(solution)/shard_map/ppermute | solution.py:243
  517.2 172.6 %collective-permute-start.63 = (bf16[96,2304]{1,0:T(8,128)(2,1)}, bf16[96,2304]{1,0:T(8,128)(2,1)}, u32[]{:S(2)}, u32[]{:S(2)}) collective-permute-start(bf16[96,2304]{1,0:T(8,128)(2,1)} %pad_maximum_fusion.29), channel_id=1, source_target_pairs={{0,2},{1,3},{2,0},{3,1},{4,6},{5,7},{6,4},{7,5},{8,10},{9,11},{10,... | collective-permute-start | bytes 1327112 | tf_op jit(solution)/shard_map/ppermute | solution.py:243
  638.9 20.2 %collective-permute-start.119 = (f32[4,12,192]{2,1,0:T(8,128)S(1)}, f32[4,12,192]{2,1,0:T(8,128)S(1)}, u32[]{:S(2)}, u32[]{:S(2)}) collective-permute-start(f32[4,12,192]{2,1,0:T(8,128)S(1)} %fusion.112), channel_id=1, source_target_pairs={{0,16},{16,0},{1,17},{17,1},{2,18},{18,2},{3,19},{19,3},{4,20},{20... | collective-permute-start | bytes 110600 | tf_op jit(solution)/shard_map/ppermute | solution.py:239
  655.6 147.4 %all-to-all-start.4 = ((bf16[1,4,256,768]{3,2,0,1:T(8,128)(2,1)}), bf16[1,4,256,768]{3,2,0,1:T(8,128)(2,1)S(1)}, u32[]{:S(2)}, u32[]{:S(2)}) async-start(bf16[1,4,256,768]{3,2,0,1:T(8,128)(2,1)} %bitcast.92), calls=%async_computation.4 | async-start | bytes 3145728 | tf_op jit(solution)/shard_map/all_to_all | solution.py:387
  669.4 48.3 %collective-permute-start.111 = (bf16[192,768]{1,0:T(8,128)(2,1)}, bf16[192,768]{1,0:T(8,128)(2,1)}, u32[]{:S(2)}, u32[]{:S(2)}) collective-permute-start(bf16[192,768]{1,0:T(8,128)(2,1)} %get-tuple-element.142), channel_id=1, source_target_pairs={{0,2},{1,3},{2,0},{3,1},{4,6},{5,7},{6,4},{7,5},{8,10},{9,11},{10,... | collective-permute-start | bytes 884744 | tf_op jit(solution)/shard_map/ppermute | solution.py:243
  687.5 31.1 %collective-permute-start.113 = (bf16[192,768]{1,0:T(8,128)(2,1)}, bf16[192,768]{1,0:T(8,128)(2,1)}, u32[]{:S(2)}, u32[]{:S(2)}) collective-permute-start(bf16[192,768]{1,0:T(8,128)(2,1)} %get-tuple-element.144), channel_id=1, source_target_pairs={{0,1},{1,0},{2,3},{3,2},{4,5},{5,4},{6,7},{7,6},{8,9},{9,8},{10,11... | collective-permute-start | bytes 884744 | tf_op jit(solution)/shard_map/ppermute | solution.py:243
  705.0 112.1 %collective-permute-start.102 = (bf16[4,384,768]{2,1,0:T(8,128)(2,1)}, bf16[4,384,768]{2,1,0:T(8,128)(2,1)}, u32[]{:S(2)}, u32[]{:S(2)}) collective-permute-start(bf16[4,384,768]{2,1,0:T(8,128)(2,1)} %select_bitcast_fusion.1), channel_id=1, source_target_pairs={{0,16},{16,0},{1,17},{17,1},{2,18},{18,2},{3,19},{19,3},{4,20},{20... | collective-permute-start | bytes 7077896 | tf_op jit(solution)/shard_map/ppermute | solution.py:239
  712.9 18.2 %collective-permute-start.64 = (bf16[96,2304]{1,0:T(8,128)(2,1)S(1)}, bf16[96,2304]{1,0:T(8,128)(2,1)S(1)}, u32[]{:S(2)}, u32[]{:S(2)}) collective-permute-start(bf16[96,2304]{1,0:T(8,128)(2,1)S(1)} %copy-done.103), channel_id=1, source_target_pairs={{0,4},{12,8},{1,5},{13,9},{2,6},{14,10},{3,7},{15,11},{16,20},{28,... | collective-permute-start | bytes 1327112 | tf_op jit(solution)/shard_map/ppermute | solution.py:289
  735.2 18.8 %collective-permute-start.112 = (bf16[384,768]{1,0:T(8,128)(2,1)S(1)}, bf16[384,768]{1,0:T(8,128)(2,1)S(1)}, u32[]{:S(2)}, u32[]{:S(2)}) collective-permute-start(bf16[384,768]{1,0:T(8,128)(2,1)S(1)} %pad_maximum_fusion.24), channel_id=1, source_target_pairs={{0,1},{1,0},{2,3},{3,2},{4,5},{5,4},{6,7},{7,6},{8,9},{9,8},{10,11... | collective-permute-start | bytes 1769480 | tf_op jit(solution)/shard_map/ppermute | solution.py:243
  747.7 75.9 %collective-permute-start.85 = (bf16[4,96,3072]{2,1,0:T(8,128)(2,1)}, bf16[4,96,3072]{2,1,0:T(8,128)(2,1)}, u32[]{:S(2)}, u32[]{:S(2)}) collective-permute-start(bf16[4,96,3072]{2,1,0:T(8,128)(2,1)} %select_bitcast_fusion.3), channel_id=1, source_target_pairs={{0,16},{16,0},{1,17},{17,1},{2,18},{18,2},{3,19},{19,3},{4,20},{20... | collective-permute-start | bytes 7077896 | tf_op jit(solution)/shard_map/ppermute | solution.py:239
  757.1 34.5 %collective-permute-start.51 = (bf16[4,96,2304]{2,1,0:T(8,128)(2,1)S(1)}, bf16[4,96,2304]{2,1,0:T(8,128)(2,1)S(1)}, u32[]{:S(2)}, u32[]{:S(2)}) collective-permute-start(bf16[4,96,2304]{2,1,0:T(8,128)(2,1)S(1)} %copy-done.102), channel_id=1, source_target_pairs={{0,16},{16,0},{1,17},{17,1},{2,18},{18,2},{3,19},{19,3},{4,20},{20... | collective-permute-start | bytes 5308424 | tf_op jit(solution)/shard_map/ppermute | solution.py:239
  766.5 26.9 %collective-permute-start.49 = (bf16[4,256,768]{2,1,0:T(8,128)(2,1)S(1)}, bf16[4,256,768]{2,1,0:T(8,128)(2,1)S(1)}, u32[]{:S(2)}, u32[]{:S(2)}) collective-permute-start(bf16[4,256,768]{2,1,0:T(8,128)(2,1)S(1)} %copy-done.105), channel_id=1, source_target_pairs={{0,16},{16,0},{1,17},{17,1},{2,18},{18,2},{3,19},{19,3},{4,20},{20... | collective-permute-start | bytes 4718600 | tf_op jit(solution)/shard_map/ppermute | solution.py:239
  789.3 117.8 %collective-permute-start.66 = (bf16[96,2304]{1,0:T(8,128)(2,1)}, bf16[96,2304]{1,0:T(8,128)(2,1)}, u32[]{:S(2)}, u32[]{:S(2)}) collective-permute-start(bf16[96,2304]{1,0:T(8,128)(2,1)} %add_convert_fusion.17), channel_id=1, source_target_pairs={{4,0},{8,12},{5,1},{9,13},{6,2},{10,14},{7,3},{11,15},{20,16},{24,... | collective-permute-start | bytes 1327112 | tf_op jit(solution)/shard_map/ppermute | solution.py:291
  803.0 57.0 %all-to-all-start.5 = ((bf16[1,4,256,768]{3,2,0,1:T(8,128)(2,1)}), bf16[1,4,256,768]{3,2,0,1:T(8,128)(2,1)S(1)}, u32[]{:S(2)}, u32[]{:S(2)}) async-start(bf16[1,4,256,768]{3,2,0,1:T(8,128)(2,1)} %bitcast.652), calls=%async_computation.5 | async-start | bytes 3145728 | tf_op jit(solution)/shard_map/all_to_all | solution.py:387
  810.6 51.1 %collective-permute-start.53 = (bf16[96,2304]{1,0:T(8,128)(2,1)}, bf16[96,2304]{1,0:T(8,128)(2,1)}, u32[]{:S(2)}, u32[]{:S(2)}) collective-permute-start(bf16[96,2304]{1,0:T(8,128)(2,1)} %pad_maximum_fusion.26), channel_id=1, source_target_pairs={{0,1},{1,0},{2,3},{3,2},{4,5},{5,4},{6,7},{7,6},{8,9},{9,8},{10,11... | collective-permute-start | bytes 1327112 | tf_op jit(solution)/shard_map/ppermute | solution.py:243
  813.5 49.0 %collective-permute-start.55 = (bf16[96,2304]{1,0:T(8,128)(2,1)}, bf16[96,2304]{1,0:T(8,128)(2,1)}, u32[]{:S(2)}, u32[]{:S(2)}) collective-permute-start(bf16[96,2304]{1,0:T(8,128)(2,1)} %pad_maximum_fusion.27), channel_id=1, source_target_pairs={{0,2},{1,3},{2,0},{3,1},{4,6},{5,7},{6,4},{7,5},{8,10},{9,11},{10,... | collective-permute-start | bytes 1327112 | tf_op jit(solution)/shard_map/ppermute | solution.py:243
  817.1 131.7 %collective-permute-start.117 = (bf16[384,768]{1,0:T(8,128)(2,1)}, bf16[384,768]{1,0:T(8,128)(2,1)}, u32[]{:S(2)}, u32[]{:S(2)}) collective-permute-start(bf16[384,768]{1,0:T(8,128)(2,1)} %add_convert_fusion.9), channel_id=1, source_target_pairs={{4,0},{8,12},{5,1},{9,13},{6,2},{10,14},{7,3},{11,15},{20,16},{24,... | collective-permute-start | bytes 1769480 | tf_op jit(solution)/shard_map/ppermute | solution.py:291
  823.6 41.4 %collective-permute-start.103 = (bf16[192,768]{1,0:T(8,128)(2,1)}, bf16[192,768]{1,0:T(8,128)(2,1)}, u32[]{:S(2)}, u32[]{:S(2)}) collective-permute-start(bf16[192,768]{1,0:T(8,128)(2,1)} %get-tuple-element.148), channel_id=1, source_target_pairs={{0,2},{1,3},{2,0},{3,1},{4,6},{5,7},{6,4},{7,5},{8,10},{9,11},{10,... | collective-permute-start | bytes 884744 | tf_op jit(solution)/shard_map/ppermute | solution.py:243
  862.5 18.1 %collective-permute-start.86 = (bf16[48,3072]{1,0:T(8,128)(2,1)S(1)}, bf16[48,3072]{1,0:T(8,128)(2,1)S(1)}, u32[]{:S(2)}, u32[]{:S(2)}) collective-permute-start(bf16[48,3072]{1,0:T(8,128)(2,1)S(1)} %get-tuple-element.160), channel_id=1, source_target_pairs={{0,2},{1,3},{2,0},{3,1},{4,6},{5,7},{6,4},{7,5},{8,10},{9,11},{10,... | collective-permute-start | bytes 884744 | tf_op jit(solution)/shard_map/ppermute | solution.py:243
  865.0 16.3 %collective-permute-start.88 = (bf16[48,3072]{1,0:T(8,128)(2,1)S(1)}, bf16[48,3072]{1,0:T(8,128)(2,1)S(1)}, u32[]{:S(2)}, u32[]{:S(2)}) collective-permute-start(bf16[48,3072]{1,0:T(8,128)(2,1)S(1)} %get-tuple-element.162), channel_id=1, source_target_pairs={{0,1},{1,0},{2,3},{3,2},{4,5},{5,4},{6,7},{7,6},{8,9},{9,8},{10,11... | collective-permute-start | bytes 884744 | tf_op jit(solution)/shard_map/ppermute | solution.py:243
  880.6 20.7 %collective-permute-start.104 = (bf16[384,768]{1,0:T(8,128)(2,1)S(1)}, bf16[384,768]{1,0:T(8,128)(2,1)S(1)}, u32[]{:S(2)}, u32[]{:S(2)}) collective-permute-start(bf16[384,768]{1,0:T(8,128)(2,1)S(1)} %pad_maximum_fusion.22), channel_id=1, source_target_pairs={{0,1},{1,0},{2,3},{3,2},{4,5},{5,4},{6,7},{7,6},{8,9},{9,8},{10,11... | collective-permute-start | bytes 1769480 | tf_op jit(solution)/shard_map/ppermute | solution.py:243
  899.8 16.7 %collective-permute-start.58 = (bf16[96,2304]{1,0:T(8,128)(2,1)S(1)}, bf16[96,2304]{1,0:T(8,128)(2,1)S(1)}, u32[]{:S(2)}, u32[]{:S(2)}) collective-permute-start(bf16[96,2304]{1,0:T(8,128)(2,1)S(1)} %add_convert_fusion.19), channel_id=1, source_target_pairs={{4,0},{8,12},{5,1},{9,13},{6,2},{10,14},{7,3},{11,15},{20,16},{24,... | collective-permute-start | bytes 1327112 | tf_op jit(solution)/shard_map/ppermute | solution.py:291
  901.3 75.4 %collective-permute-start.100 = (bf16[96,3072]{1,0:T(8,128)(2,1)S(1)}, bf16[96,3072]{1,0:T(8,128)(2,1)S(1)}, u32[]{:S(2)}, u32[]{:S(2)}) collective-permute-start(bf16[96,3072]{1,0:T(8,128)(2,1)S(1)} %copy-done.96), channel_id=1, source_target_pairs={{4,0},{8,12},{5,1},{9,13},{6,2},{10,14},{7,3},{11,15},{20,16},{24,... | collective-permute-start | bytes 1769480 | tf_op jit(solution)/shard_map/ppermute | solution.py:291
  906.9 36.3 %collective-permute-start.50 = (bf16[4,256,768]{2,1,0:T(8,128)(2,1)S(1)}, bf16[4,256,768]{2,1,0:T(8,128)(2,1)S(1)}, u32[]{:S(2)}, u32[]{:S(2)}) collective-permute-start(bf16[4,256,768]{2,1,0:T(8,128)(2,1)S(1)} %fusion.75), channel_id=1, source_target_pairs={{0,16},{16,0},{1,17},{17,1},{2,18},{18,2},{3,19},{19,3},{4,20},{20... | collective-permute-start | bytes 4718600 | tf_op jit(solution)/shard_map/ppermute | solution.py:239
  907.1 23.0 %collective-permute-start.107 = (bf16[384,768]{1,0:T(8,128)(2,1)S(1)}, bf16[384,768]{1,0:T(8,128)(2,1)S(1)}, u32[]{:S(2)}, u32[]{:S(2)}) collective-permute-start(bf16[384,768]{1,0:T(8,128)(2,1)S(1)} %fusion.81), channel_id=1, source_target_pairs={{0,4},{12,8},{1,5},{13,9},{2,6},{14,10},{3,7},{15,11},{16,20},{28,... | collective-permute-start | bytes 1769480 | tf_op jit(solution)/shard_map/ppermute | solution.py:289
  916.5 25.8 %collective-permute-start.90 = (bf16[96,3072]{1,0:T(8,128)(2,1)S(1)}, bf16[96,3072]{1,0:T(8,128)(2,1)S(1)}, u32[]{:S(2)}, u32[]{:S(2)}) collective-permute-start(bf16[96,3072]{1,0:T(8,128)(2,1)S(1)} %fusion.85), channel_id=1, source_target_pairs={{0,4},{12,8},{1,5},{13,9},{2,6},{14,10},{3,7},{15,11},{16,20},{28,... | collective-permute-start | bytes 1769480 | tf_op jit(solution)/shard_map/ppermute | solution.py:289
  930.1 18.6 %collective-permute-start.67 = (bf16[96,2304]{1,0:T(8,128)(2,1)S(1)}, bf16[96,2304]{1,0:T(8,128)(2,1)S(1)}, u32[]{:S(2)}, u32[]{:S(2)}) collective-permute-start(bf16[96,2304]{1,0:T(8,128)(2,1)S(1)} %get-tuple-element.118), channel_id=1, source_target_pairs={{0,16},{16,0},{1,17},{17,1},{2,18},{18,2},{3,19},{19,3},{4,20},{20... | collective-permute-start | bytes 1327112 | tf_op jit(solution)/shard_map/ppermute | solution.py:239
  945.9 29.5 %collective-permute-start.109 = (bf16[384,768]{1,0:T(8,128)(2,1)S(1)}, bf16[384,768]{1,0:T(8,128)(2,1)S(1)}, u32[]{:S(2)}, u32[]{:S(2)}) collective-permute-start(bf16[384,768]{1,0:T(8,128)(2,1)S(1)} %add_convert_fusion.11), channel_id=1, source_target_pairs={{4,0},{8,12},{5,1},{9,13},{6,2},{10,14},{7,3},{11,15},{20,16},{24,... | collective-permute-start | bytes 1769480 | tf_op jit(solution)/shard_map/ppermute | solution.py:291
  947.4 40.6 %collective-permute-start.92 = (bf16[96,3072]{1,0:T(8,128)(2,1)S(1)}, bf16[96,3072]{1,0:T(8,128)(2,1)S(1)}, u32[]{:S(2)}, u32[]{:S(2)}) collective-permute-start(bf16[96,3072]{1,0:T(8,128)(2,1)S(1)} %add_convert_fusion.15), channel_id=1, source_target_pairs={{4,0},{8,12},{5,1},{9,13},{6,2},{10,14},{7,3},{11,15},{20,16},{24,... | collective-permute-start | bytes 1769480 | tf_op jit(solution)/shard_map/ppermute | solution.py:291
  (242 other events, 2550.1 us)
